TPU v7x, 256 devices: a whole 4x4x8 slice. The times are simulated.
256 devices in a mesh: sec: 2 (over y_lo), gx: 8 (over y_hi, x), gy: 16 (over z, core).
Axes of the slice: x: 4, y: 4 (y_hi: 2, y_lo: 2; y = y_hi * 2 + y_lo), z: 8, core: 2. Of those that a mesh axis runs over, the one named last changes fastest.
Arguments:
- state: float32 [2, 3, 8, 16, 102400], P('sec', None, 'gx', 'gy'), may hold values from -6 to 6
- previous: float32 [2, 3, 8, 16, 102400], P('sec', None, 'gx', 'gy'), may hold values from -6 to 6
- coeff: float32 [2, 2, 8, 16, 102400], P('sec', None, 'gx', 'gy'), may hold values from 0.04 to 0.16
- wet_mask: int32 [8, 16, 102400], P('gx', 'gy'), may hold values 0 or 1
- link_dest: int32 [2, 8, 16, 256, 1], P('sec', 'gx', 'gy'), may hold values from 0 to 127; in each aligned block of 256 rows (0 to 255, 256 to 511, ..., all dimensions but the last counted through in order) at most 4 rows name the same one
- link_rows: int32 [2, 8, 16, 256, 2], P('sec', 'gx', 'gy'), may hold values from 0 to 79, as said below
- link_weight: float32 [2, 8, 16, 256], P('sec', 'gx', 'gy'), may hold values from 0.5 to 2
Outputs:
- final_state: float32 [2, 3, 8, 16, 102400], P('sec', None, 'gx', 'gy')
Inputs may be any that keep to these rules, and one draw needn't show every extreme that they name: `link_rows`: in section 0, [..., 0] lies below 8 and [..., 1] below 80; in section 1, [..., 0] lies below 80 and [..., 1] below 8. `link_dest`: among the 256 links of one device at most 4 name the same owner.
All inputs are finite; a program needn't handle non-finite values. No bound on the sum of `wet_mask` on one device may be relied on, other than what follows from the above.
Results may differ from a plain program's by a relative error of at most 0.0001.
Values sent between devices are 32-bit elements; how exact they have to be, the bound alone decides.
A program may use at most 128 MiB of HBM per device.

v0:
```python
import functools

import jax
import jax.numpy as jnp
from jax import lax
from jax.experimental import pallas as pl
from jax.experimental.pallas import tpu as pltpu
from jax.sharding import PartitionSpec as P

CX = 8
CY = 128
REFINE = 10
NL = 100
STEPS = 4
CAP = 4

ROWS = CX * NL
BASE = 104
PAD_ROWS = BASE + ROWS + BASE
CHUNK = 40
EDGE = 16
HALO_ROWS = NL + 4
EDGE_LANES = 896


def from_partner(value, axis, stride):
    return lax.ppermute(value, axis, [(i, i ^ 1 << stride) for i in range(lax.axis_size(axis))])


def shift_pairs(axis):
    count = lax.axis_size(axis)
    forward = [(i, i + 1) for i in range(count - 1)]
    backward = [(target, source) for source, target in forward]
    return forward, backward


def fill_scratch(scratch, cur_ref, low_ref, high_ref, fields):
    for f in range(fields):
        scratch[f, pl.ds(BASE - HALO_ROWS, HALO_ROWS), :] = low_ref[f]
        scratch[f, pl.ds(BASE, ROWS), :] = cur_ref[f]
        scratch[f, pl.ds(BASE + ROWS, HALO_ROWS), :] = high_ref[f]


def lane_index(rows):
    return lax.broadcasted_iota(jnp.int32, (rows, CY), 1)


def row_mask(r0, rows, period, phase):
    local = lax.broadcasted_iota(jnp.int32, (rows, CY), 0)
    mask = jnp.zeros((rows, CY), jnp.bool_)
    for r in range(rows):
        if (r0 + r) % period == phase:
            mask = mask | (local == r)
    return mask


def exact_dot(a, b):
    return jnp.dot(a, b, precision=lax.Precision.HIGHEST, preferred_element_type=jnp.float32)


def select_dot(a, b):
    return jnp.dot(a, b, precision=lax.Precision.HIGH, preferred_element_type=jnp.float32)


def landing_sum(rows_ref, arrived_ref, count):
    slots = rows_ref.shape[1]
    one_hot = (lax.broadcasted_iota(jnp.int32, (count, slots), 0) == rows_ref[...]).astype(jnp.float32)
    return exact_dot(one_hot, arrived_ref[...])


def edge_rows(out_ref, edges_ref):
    rows = lax.broadcasted_iota(jnp.int32, (8, CY), 0)
    lanes = lax.broadcasted_iota(jnp.int32, (8, CY), 1)
    select = (((rows == 0) & (lanes == CY - 1)) | ((rows == 1) & (lanes == 0))).astype(jnp.float32)
    for f in range(3):
        picked = lax.dot_general(select, out_ref[f], (((1,), (1,)), ((), ())), precision=lax.Precision.HIGHEST,
                                 preferred_element_type=jnp.float32)
        edges_ref[f] = jnp.zeros(edges_ref.shape[1:], jnp.float32)
        edges_ref[f, :, pl.ds(0, ROWS)] = picked


def fill_sides(low_rows_ref, high_rows_ref, left_pad, right_pad):
    for f in range(3):
        left_pad[f, pl.ds(EDGE, ROWS), :] = jnp.transpose(low_rows_ref[f])[:ROWS, 0:1]
        right_pad[f, pl.ds(EDGE, ROWS), :] = jnp.transpose(high_rows_ref[f])[:ROWS, 1:2]


def spread(cb):
    coarse = lax.broadcasted_iota(jnp.int32, (CY, CY), 0)
    fine = lax.broadcasted_iota(jnp.int32, (CY, CY), 1) + cb * CY
    return ((fine >= coarse * REFINE) & (fine < coarse * REFINE + REFINE)).astype(jnp.float32)


def elastic_kernel(cur_ref, prev_ref, coef_ref, low_ref, high_ref, low_rows_ref, high_rows_ref, rows_ref, arrived_ref,
                   pick_ref, out_ref, tiles_ref, edges_ref, scratch, left_pad, right_pad):
    fill_scratch(scratch, cur_ref, low_ref, high_ref, 3)
    fill_sides(low_rows_ref, high_rows_ref, left_pad, right_pad)
    force = landing_sum(rows_ref, arrived_ref, CX)
    lanes = lane_index(CHUNK)
    first_lane = lanes == 0
    last_lane = lanes == CY - 1
    own_axis = (0, 2, 1)
    for r0 in range(0, ROWS, CHUNK):
        top_layer = row_mask(r0, CHUNK, NL, 0)
        bottom_layer = row_mask(r0, CHUNK, NL, NL - 1)
        shear = coef_ref[0, pl.ds(r0, CHUNK), :]
        lame = coef_ref[1, pl.ds(r0, CHUNK), :]
        stiffness = lame + 2.0 * shear
        for c in range(3):
            at = BASE + r0
            v = scratch[c, pl.ds(at, CHUNK), :]
            along_first = scratch[c, pl.ds(at + NL, CHUNK), :] - 2.0 * v + scratch[c, pl.ds(at - NL, CHUNK), :]
            deeper = jnp.where(bottom_layer, 0.0, scratch[c, pl.ds(at + 1, CHUNK), :])
            shallower = jnp.where(top_layer, 0.0, scratch[c, pl.ds(at - 1, CHUNK), :])
            along_depth = deeper - 2.0 * v + shallower
            after = jnp.where(last_lane, right_pad[c, pl.ds(EDGE + r0, CHUNK), :], pltpu.roll(v, CY - 1, 1))
            before = jnp.where(first_lane, left_pad[c, pl.ds(EDGE + r0, CHUNK), :], pltpu.roll(v, 1, 1))
            along_second = after - 2.0 * v + before
            factors = [stiffness if own_axis[c] == axis_index else shear for axis_index in range(3)]
            acceleration = factors[0] * along_first + factors[1] * along_depth + factors[2] * along_second
            out_ref[c, pl.ds(r0, CHUNK), :] = 2.0 * v - prev_ref[c, pl.ds(r0, CHUNK), :] + acceleration
    for x in range(CX):
        out_ref[2, pl.ds(x * NL, 1), :] = out_ref[2, pl.ds(x * NL, 1), :] + force[x : x + 1]
    elastic_tiles(out_ref, pick_ref, tiles_ref)
    edge_rows(out_ref, edges_ref)


def shallow_kernel(cur_ref, prev_ref, coef_ref, wet_ref, low_ref, high_ref, low_rows_ref, high_rows_ref, rows_ref,
                   arrived_ref, pick_ref, out_ref, tiles_ref, edges_ref, scratch, source_ref, left_pad, right_pad):
    fill_scratch(scratch, cur_ref, low_ref, high_ref, 3)
    fill_sides(low_rows_ref, high_rows_ref, left_pad, right_pad)
    coarse_source = landing_sum(rows_ref, arrived_ref, REFINE * CX)
    for cb in range(REFINE):
        source_ref[pl.ds(cb, REFINE * CX, stride=REFINE), :] = select_dot(coarse_source, spread(cb))
    lanes = lane_index(CHUNK)
    first_lane = lanes == 0
    last_lane = lanes == CY - 1
    first_block = row_mask(0, CHUNK, REFINE, 0)
    last_block = row_mask(0, CHUNK, REFINE, REFINE - 1)
    for r0 in range(0, ROWS, CHUNK):
        at = BASE + r0

        def rows_diff(f):
            return scratch[f, pl.ds(at + REFINE, CHUNK), :] - scratch[f, pl.ds(at - REFINE, CHUNK), :]

        def columns_diff(f):
            v = scratch[f, pl.ds(at, CHUNK), :]
            wrap_after = jnp.where(last_block, right_pad[f, pl.ds(EDGE + r0 - (REFINE - 1), CHUNK), :],
                                   pltpu.roll(scratch[f, pl.ds(at + 1, CHUNK), :], CY - 1, 1))
            wrap_before = jnp.where(first_block, left_pad[f, pl.ds(EDGE + r0 + REFINE - 1, CHUNK), :],
                                    pltpu.roll(scratch[f, pl.ds(at - 1, CHUNK), :], 1, 1))
            after = jnp.where(last_lane, wrap_after, pltpu.roll(v, CY - 1, 1))
            before = jnp.where(first_lane, wrap_before, pltpu.roll(v, 1, 1))
            return after - before

        wave = coef_ref[0, pl.ds(r0, CHUNK), :]
        area = coef_ref[1, pl.ds(r0, CHUNK), :]
        wet = wet_ref[pl.ds(r0, CHUNK), :].astype(jnp.float32)
        eta_r = rows_diff(0)
        eta_c = columns_diff(0)
        out_ref[1, pl.ds(r0, CHUNK), :] = wet * (prev_ref[1, pl.ds(r0, CHUNK), :] - wave * eta_r)
        out_ref[2, pl.ds(r0, CHUNK), :] = wet * (prev_ref[2, pl.ds(r0, CHUNK), :] - wave * eta_c)
        divergence = rows_diff(1) + columns_diff(2)
        out_ref[0, pl.ds(r0, CHUNK), :] = wet * (
            prev_ref[0, pl.ds(r0, CHUNK), :] - area * divergence + source_ref[pl.ds(r0, CHUNK), :]
        )
    shallow_tiles(out_ref, pick_ref, tiles_ref)
    edge_rows(out_ref, edges_ref)


def shallow_tiles(field_ref, pick_ref, tiles_ref):
    total = jnp.zeros((REFINE * CX, CY), jnp.float32)
    for cb in range(REFINE):
        total = total + select_dot(field_ref[0, pl.ds(cb, REFINE * CX, stride=REFINE), :], spread(cb).T)
    tiles_ref[...] = exact_dot(pick_ref[...], total / REFINE)


def elastic_tiles(field_ref, pick_ref, tiles_ref):
    uplift = field_ref[2, pl.ds(0, CX, stride=NL), :]
    tiles_ref[...] = exact_dot(pick_ref[:, :CX], uplift)


def prepare_kernel(tiles_of, cur_ref, pick_ref, tiles_ref, edges_ref):
    tiles_of(cur_ref, pick_ref, tiles_ref)
    edge_rows(cur_ref, edges_ref)


def prepare(tiles_of, current, pick):
    return pl.pallas_call(
        functools.partial(prepare_kernel, tiles_of),
        out_shape=(
            jax.ShapeDtypeStruct((pick.shape[0], CY), jnp.float32),
            jax.ShapeDtypeStruct((3, 8, EDGE_LANES), jnp.float32),
        ),
        in_specs=vmem_specs(2),
        out_specs=tuple(vmem_specs(2)),
    )(current, pick)


def vmem_specs(count):
    return [pl.BlockSpec(memory_space=pltpu.VMEM)] * count


def run_step(kernel, scratch_shapes, *operands):
    slots = operands[-1].shape[0]
    return pl.pallas_call(
        kernel,
        out_shape=(
            jax.ShapeDtypeStruct((3, ROWS, CY), jnp.float32),
            jax.ShapeDtypeStruct((slots, CY), jnp.float32),
            jax.ShapeDtypeStruct((3, 8, EDGE_LANES), jnp.float32),
        ),
        in_specs=vmem_specs(len(operands)),
        out_specs=tuple(vmem_specs(3)),
        scratch_shapes=scratch_shapes,
    )(*operands)


def exchange_kernel(sizes, cur_ref, edges_ref, out_ref, in_ref, low_ref, high_ref, low_rows_ref, high_rows_ref,
                    land, halo, sides, send_sem, recv_sem, halo_send, halo_recv, side_send, side_recv):
    owners, rows_of, columns = sizes
    other = 1 - lax.axis_index("sec")
    section = lax.axis_index("sec")
    gx = lax.axis_index("gx")
    gy = lax.axis_index("gy")
    me = gx * columns + gy
    has_low = gx > 0
    has_high = gx < rows_of - 1
    has_left = gy > 0
    has_right = gy < columns - 1
    halo[...] = jnp.zeros_like(halo)
    sides[...] = jnp.zeros_like(sides)
    barrier = pltpu.get_barrier_semaphore()
    def greet(d, carry):
        pl.semaphore_signal(barrier, inc=1, device_id=(other, d // columns, d % columns),
                            device_id_type=pl.DeviceIdType.MESH)
        return carry

    lax.fori_loop(0, owners, greet, 0, unroll=8)

    @pl.when(has_low)
    def _():
        pl.semaphore_signal(barrier, inc=1, device_id=(section, gx - 1, gy), device_id_type=pl.DeviceIdType.MESH)

    @pl.when(has_high)
    def _():
        pl.semaphore_signal(barrier, inc=1, device_id=(section, gx + 1, gy), device_id_type=pl.DeviceIdType.MESH)

    @pl.when(has_left)
    def _():
        pl.semaphore_signal(barrier, inc=1, device_id=(section, gx, gy - 1), device_id_type=pl.DeviceIdType.MESH)

    @pl.when(has_right)
    def _():
        pl.semaphore_signal(barrier, inc=1, device_id=(section, gx, gy + 1), device_id_type=pl.DeviceIdType.MESH)

    neighbours = [has_low, has_high, has_left, has_right]
    pl.semaphore_wait(barrier, owners + sum(n.astype(jnp.int32) for n in neighbours))

    def side_copy(slot, target):
        return pltpu.make_async_remote_copy(
            src_ref=edges_ref,
            dst_ref=sides.at[slot],
            send_sem=side_send.at[slot],
            recv_sem=side_recv.at[slot],
            device_id=(section, gx, target),
            device_id_type=pl.DeviceIdType.MESH,
        )

    @pl.when(has_right)
    def _():
        side_copy(0, gy + 1).start()

    @pl.when(has_left)
    def _():
        side_copy(1, gy - 1).start()

    def slab_copy(start, slot, target):
        return pltpu.make_async_remote_copy(
            src_ref=cur_ref.at[:, pl.ds(start, HALO_ROWS), :],
            dst_ref=halo.at[slot],
            send_sem=halo_send.at[slot],
            recv_sem=halo_recv.at[slot],
            device_id=(section, target, gy),
            device_id_type=pl.DeviceIdType.MESH,
        )

    @pl.when(has_high)
    def _():
        slab_copy(ROWS - HALO_ROWS, 0, gx + 1).start()

    @pl.when(has_low)
    def _():
        slab_copy(0, 1, gx - 1).start()

    def send(d, carry):
        pltpu.make_async_remote_copy(
            src_ref=out_ref.at[pl.ds(d * CAP, CAP)],
            dst_ref=land.at[pl.ds(me * CAP, CAP)],
            send_sem=send_sem,
            recv_sem=recv_sem,
            device_id=(other, d // columns, d % columns),
            device_id_type=pl.DeviceIdType.MESH,
        ).start()
        return carry

    lax.fori_loop(0, owners, send, 0, unroll=8)
    whole = pltpu.make_async_remote_copy(
        src_ref=out_ref,
        dst_ref=land,
        send_sem=send_sem,
        recv_sem=recv_sem,
        device_id=(other, gx, gy),
        device_id_type=pl.DeviceIdType.MESH,
    )

    @pl.when(has_high)
    def _():
        slab_copy(ROWS - HALO_ROWS, 0, gx + 1).wait_send()
        slab_copy(0, 1, gx + 1).wait_recv()

    @pl.when(has_low)
    def _():
        slab_copy(0, 1, gx - 1).wait_send()
        slab_copy(ROWS - HALO_ROWS, 0, gx - 1).wait_recv()

    @pl.when(has_right)
    def _():
        side_copy(0, gy + 1).wait_send()
        side_copy(1, gy + 1).wait_recv()

    @pl.when(has_left)
    def _():
        side_copy(1, gy - 1).wait_send()
        side_copy(0, gy - 1).wait_recv()

    whole.wait_send()
    whole.wait_recv()
    in_ref[...] = land[...]
    low_ref[...] = halo[0]
    high_ref[...] = halo[1]
    low_rows_ref[...] = sides[0]
    high_rows_ref[...] = sides[1]


def exchange(current, edges, outgoing, owners, rows_of, columns):
    halo_shape = jax.ShapeDtypeStruct((3, HALO_ROWS, CY), jnp.float32)
    side_shape = jax.ShapeDtypeStruct(edges.shape, jnp.float32)
    return pl.pallas_call(
        functools.partial(exchange_kernel, (owners, rows_of, columns)),
        out_shape=(jax.ShapeDtypeStruct(outgoing.shape, jnp.float32), halo_shape, halo_shape, side_shape, side_shape),
        in_specs=[pl.BlockSpec(memory_space=pl.ANY)] * 2 + [pl.BlockSpec(memory_space=pltpu.VMEM)],
        out_specs=tuple(vmem_specs(5)),
        scratch_shapes=[
            pltpu.VMEM(outgoing.shape, jnp.float32),
            pltpu.VMEM((2, 3, HALO_ROWS, CY), jnp.float32),
            pltpu.VMEM((2,) + edges.shape, jnp.float32),
            pltpu.SemaphoreType.DMA(()),
            pltpu.SemaphoreType.DMA(()),
            pltpu.SemaphoreType.DMA((2,)),
            pltpu.SemaphoreType.DMA((2,)),
            pltpu.SemaphoreType.DMA((2,)),
            pltpu.SemaphoreType.DMA((2,)),
        ],
        compiler_params=pltpu.CompilerParams(collective_id=0, has_side_effects=True),
    )(current, edges, outgoing)


def route(payload):
    tile_data, tile_rows = payload
    width = tile_data.shape[-1]
    received_data, received_rows = (
        lax.all_to_all(tile_data, ("gx", "gy"), split_axis=0, concat_axis=0, tiled=True),
        lax.all_to_all(tile_rows, ("gx", "gy"), split_axis=0, concat_axis=0, tiled=True),
    )
    return (received_data.reshape(-1, width), received_rows.reshape(-1))


def deliver(outgoing, send_rows):
    routed = route((outgoing, send_rows))
    return from_partner((routed[0], routed[1]), "sec", 0)


def on_device(state, previous, coeff, wet_mask, link_dest, link_rows, link_weight):
    section = lax.axis_index("sec")
    owners = lax.axis_size("gx") * lax.axis_size("gy")
    fine_rows = REFINE * CX
    current = state[0, :, 0, 0].reshape(3, ROWS, CY)
    earlier = previous[0, :, 0, 0].reshape(3, ROWS, CY)
    factors = coeff[0, :, 0, 0].reshape(2, ROWS, CY)
    wet = wet_mask[0, 0].reshape(ROWS, CY)
    targets = link_dest.reshape(-1)
    pairs = link_rows.reshape(-1, 2)
    source_rows = pairs[:, 0]
    landing = pairs[:, 1]
    weights = link_weight.reshape(-1)
    one_hot = (targets[:, None] == jnp.arange(owners, dtype=jnp.int32)[None, :]).astype(jnp.int32)
    before = jnp.cumsum(one_hot, axis=0) - one_hot
    slot_index = jnp.sum(before * one_hot, axis=1)
    position = targets * CAP + slot_index
    send_rows = jnp.zeros((owners * CAP,), jnp.int32).at[position].set(landing).reshape(owners, CAP)
    slot_rows = jnp.full((owners * CAP,), -1, jnp.int32).at[position].set(source_rows)
    slot_weights = jnp.zeros((owners * CAP,), jnp.float32).at[position].set(weights)
    pick = jnp.where(slot_rows[:, None] == jnp.arange(fine_rows, dtype=jnp.int32)[None, :], slot_weights[:, None], 0.0)
    arrived_rows = deliver(jnp.zeros((owners, CAP, CY), jnp.float32), send_rows)[1].reshape(1, -1)
    outgoing, edges = lax.cond(
        section == 0,
        lambda: prepare(elastic_tiles, current, pick),
        lambda: prepare(shallow_tiles, current, pick),
    )
    for step_index in range(STEPS):
        arrived, low_x, high_x, low_y, high_y = exchange(
            current, edges, outgoing, owners, lax.axis_size("gx"), lax.axis_size("gy")
        )

        def elastic_branch():
            scratch = [
                pltpu.VMEM((3, PAD_ROWS, CY), jnp.float32),
                pltpu.VMEM((3, ROWS + 2 * EDGE, 1), jnp.float32),
                pltpu.VMEM((3, ROWS + 2 * EDGE, 1), jnp.float32),
            ]
            return run_step(elastic_kernel, scratch, current, earlier, factors, low_x, high_x, low_y, high_y,
                            arrived_rows, arrived, pick)

        def shallow_branch():
            scratch = [
                pltpu.VMEM((3, PAD_ROWS, CY), jnp.float32),
                pltpu.VMEM((ROWS, CY), jnp.float32),
                pltpu.VMEM((3, ROWS + 2 * EDGE, 1), jnp.float32),
                pltpu.VMEM((3, ROWS + 2 * EDGE, 1), jnp.float32),
            ]
            return run_step(shallow_kernel, scratch, current, earlier, factors, wet, low_x, high_x, low_y, high_y,
                            arrived_rows, arrived, pick)

        updated, outgoing, edges = lax.cond(section == 0, elastic_branch, shallow_branch)
        earlier, current = (current, updated)
    return current.reshape(1, 3, 1, 1, -1)


def solution(mesh):
    placed = (
        P("sec", None, "gx", "gy", None),
        P("sec", None, "gx", "gy", None),
        P("sec", None, "gx", "gy", None),
        P("gx", "gy", None),
        P("sec", "gx", "gy", None, None),
        P("sec", "gx", "gy", None, None),
        P("sec", "gx", "gy", None),
    )
    return jax.shard_map(
        on_device,
        mesh=mesh,
        in_specs=placed,
        out_specs=P("sec", None, "gx", "gy", None),
        check_vma=False,
    )
```

profile of v0, /device:TPU:31, one launch (start us, length us, event | category | flops | bytes accessed | tf_op | source)
XLA Modules:
  0.0 139.1 jit_solution(11516623956683692643)
XLA Ops:
  0.0 0.0 copy-start
  0.0 0.8 fusion.12
  0.8 0.8 copy.15
  1.6 0.2 fusion.1
  1.9 0.9 fusion.3
  2.8 0.7 compare_select_fusion
  3.4 1.4 %scatter_custom_fusion.2 = s32[512]{0:T(512)S(1)} fusion(s32[256]{0:T(256)S(1)} %bitcast.72, s32[256]{0:T(256)S(1)} %bitcast.76, s32[]{:T(128)} %constant.9.clone.1), kind=kCustom, calls=%fused_computation.17 | custom fusion | bytes 2052 | tf_op jit(solution)/shard_map/scatter | solution.py:401
  4.8 0.7 all_to_all.6
  5.6 16.1 %all-to-all-start = ((s32[128,1,4]{2,1,0:T(1,128)}), s32[128,1,4]{2,1,0:T(1,128)S(1)}, u32[]{:S(2)}, u32[]{:S(2)}) async-start(s32[128,1,4]{2,1,0:T(1,128)} %bitcast.18), calls=%async_computation | async-start | bytes 131072 | tf_op jit(solution)/shard_map/all_to_all | solution.py:374
  21.7 1.4 %scatter_custom_fusion = s32[512]{0:T(512)S(1)} fusion(s32[256]{0:T(256)S(1)} %bitcast.73, s32[256]{0:T(256)S(1)} %bitcast.75, s32[]{:T(128)} %constant.10.clone.1), kind=kCustom, calls=%fused_computation.21 | custom fusion | bytes 2052 | tf_op jit(solution)/shard_map/scatter | solution.py:402
  23.1 1.6 %scatter_custom_fusion.1 = f32[512]{0:T(512)S(1)} fusion(s32[256]{0:T(256)S(1)} %bitcast.74, f32[256]{0:T(256)} %bitcast.79, f32[]{:T(128)} %constant.22.clone.1), kind=kCustom, calls=%fused_computation.19 | custom fusion | bytes 2560 | tf_op jit(solution)/shard_map/scatter | solution.py:403
  24.7 4.2 %all-to-all-done = s32[128,1,4]{2,1,0:T(1,128)S(1)} async-done(((s32[128,1,4]{2,1,0:T(1,128)}), s32[128,1,4]{2,1,0:T(1,128)S(1)}, u32[]{:S(2)}, u32[]{:S(2)}) %all-to-all-start) | async-done | bytes 2080 | tf_op jit(solution)/shard_map/all_to_all | solution.py:374
  28.9 0.5 broadcast.56
  29.4 0.8 reduce.3
  30.2 0.1 reshape.71
  30.3 0.6 collective-permute-start
  30.9 0.2 fusion
  31.1 0.0 copy-done
  31.1 2.9 %conditional.5 = ((f32[512,128]{1,0:T(8,128)S(1)}, f32[3,8,896]{2,1,0:T(8,128)S(1)})) conditional(s32[]{:T(128)} %convert_element_type.14, (f32[3,800,128]{2,1,0:T(8,128)S(1)}, f32[512,80]{1,0:T(8,128)S(1)}) %tuple.67, (f32[3,800,128]{2,1,0:T(8,128)S(1)}, f32[512,80]{1,0:T(8,128)S(1)}) %tuple.68), branch_computations={%region_5.6_spmd, %region_6.7_spmd} | conditional | bytes 8 | solution.py:406
  31.1 2.9 %branch_0_fun.5 = (f32[512,128]{1,0:T(8,128)S(1)}, f32[3,8,896]{2,1,0:T(8,128)S(1)}) custom-call(f32[3,800,128]{2,1,0:T(8,128)S(1)} %get-tuple-element.184.cur_ref, f32[512,80]{1,0:T(8,128)S(1)} %get-tuple-element.185.pick_ref), custom_call_target="tpu_custom_call" | custom-call | tf_op jit(solution)/shard_map/cond/branch_0_fun/pallas_call | solution.py:189
  34.0 0.0 copy-start.1
  34.0 20.8 %shard_map.75 = (f32[512,128]{1,0:T(8,128)}, f32[3,104,128]{2,1,0:T(8,128)}, f32[3,104,128]{2,1,0:T(8,128)}, f32[3,8,896]{2,1,0:T(8,128)}, f32[3,8,896]{2,1,0:T(8,128)}) custom-call(f32[3,800,128]{2,1,0:T(8,128)S(1)} %bitcast.38, f32[3,8,896]{2,1,0:T(8,128)S(1)} %get-tuple-element.305.edges_ref, f32[512,128]{1,0:T(8,128)S(1)} %get-tuple-element.306.out_ref), custom_call_target="tpu_custom_call" | custom-call | tf_op jit(solution)/shard_map/pallas_call | solution.py:349
  54.8 0.0 collective-permute-done
  54.8 0.0 copy-done.1
  54.8 6.5 %conditional.6 = ((f32[3,800,128]{2,1,0:T(8,128)S(1)}, f32[512,128]{1,0:T(8,128)}, f32[3,8,896]{2,1,0:T(8,128)})) conditional(s32[]{:T(128)} %convert_element_type.14, (f32[3,800,128]{2,1,0:T(8,128)S(1)}, f32[3,800,128]{2,1,0:T(8,128)}, f32[2,800,128]{2,1,0:T(8,128)S(1)}, s32[800,128]{1,0:T(8,128)}, f32[3,104,128]{2,1,0:T(8,128)}, ...), branch_computations={%region_8.9_spmd, %region_9.10_spmd} | conditional | bytes 8 | solution.py:435
  55.0 6.3 %branch_0_fun.6 = (f32[3,800,128]{2,1,0:T(8,128)S(1)}, f32[512,128]{1,0:T(8,128)}, f32[3,8,896]{2,1,0:T(8,128)}) custom-call(f32[3,800,128]{2,1,0:T(8,128)S(1)} %get-tuple-element.188.cur_ref, f32[3,800,128]{2,1,0:T(8,128)} %get-tuple-element.189.prev_ref, f32[2,800,128]{2,1,0:T(8,128)S(1)} %get-tuple-element.190.coef_ref, ...), custom_call_target="tpu_custom_call" | custom-call | tf_op jit(solution)/shard_map/cond/branch_0_fun/pallas_call | solution.py:206
  61.3 20.0 %shard_map.76 = (f32[512,128]{1,0:T(8,128)}, f32[3,104,128]{2,1,0:T(8,128)}, f32[3,104,128]{2,1,0:T(8,128)}, f32[3,8,896]{2,1,0:T(8,128)}, f32[3,8,896]{2,1,0:T(8,128)}) custom-call(f32[3,800,128]{2,1,0:T(8,128)S(1)} %get-tuple-element.312.cur_ref, f32[3,8,896]{2,1,0:T(8,128)} %get-tuple-element.313.edges_ref, f32[512,128]{1,0:T(8,128)} %get-tuple-element.314.out_ref), custom_call_target="tpu_custom_call" | custom-call | tf_op jit(solution)/shard_map/pallas_call | solution.py:349
  81.3 6.0 %conditional.7 = ((f32[3,800,128]{2,1,0:T(8,128)}, f32[512,128]{1,0:T(8,128)}, f32[3,8,896]{2,1,0:T(8,128)})) conditional(s32[]{:T(128)} %convert_element_type.14, (f32[3,800,128]{2,1,0:T(8,128)S(1)}, f32[3,800,128]{2,1,0:T(8,128)S(1)}, f32[2,800,128]{2,1,0:T(8,128)S(1)}, s32[800,128]{1,0:T(8,128)}, f32[3,104,128]{2,1,0:T(8,128)}, ...), branch_computations={%region_10.11_spmd, %region_11.12_spmd} | conditional | bytes 8 | solution.py:435
  81.3 6.0 %branch_0_fun.7 = (f32[3,800,128]{2,1,0:T(8,128)}, f32[512,128]{1,0:T(8,128)}, f32[3,8,896]{2,1,0:T(8,128)}) custom-call(f32[3,800,128]{2,1,0:T(8,128)S(1)} %get-tuple-element.209.cur_ref, f32[3,800,128]{2,1,0:T(8,128)S(1)} %get-tuple-element.210.prev_ref, f32[2,800,128]{2,1,0:T(8,128)S(1)} %get-tuple-element.211.coef_ref, ...), custom_call_target="tpu_custom_call" | custom-call | tf_op jit(solution)/shard_map/cond/branch_0_fun/pallas_call | solution.py:206
  87.3 0.0 copy-start.2
  87.3 20.0 %shard_map.77 = (f32[512,128]{1,0:T(8,128)}, f32[3,104,128]{2,1,0:T(8,128)}, f32[3,104,128]{2,1,0:T(8,128)}, f32[3,8,896]{2,1,0:T(8,128)}, f32[3,8,896]{2,1,0:T(8,128)}) custom-call(f32[3,800,128]{2,1,0:T(8,128)} %get-tuple-element.320.cur_ref, f32[3,8,896]{2,1,0:T(8,128)} %get-tuple-element.321.edges_ref, f32[512,128]{1,0:T(8,128)} %get-tuple-element.322.out_ref), custom_call_target="tpu_custom_call" | custom-call | tf_op jit(solution)/shard_map/pallas_call | solution.py:349
  107.3 0.0 copy-done.2
  107.3 6.0 %conditional.8 = ((f32[3,800,128]{2,1,0:T(8,128)}, f32[512,128]{1,0:T(8,128)}, f32[3,8,896]{2,1,0:T(8,128)})) conditional(s32[]{:T(128)} %convert_element_type.14, (f32[3,800,128]{2,1,0:T(8,128)S(1)}, f32[3,800,128]{2,1,0:T(8,128)S(1)}, f32[2,800,128]{2,1,0:T(8,128)S(1)}, s32[800,128]{1,0:T(8,128)}, f32[3,104,128]{2,1,0:T(8,128)}, ...), branch_computations={%region_12.13_spmd, %region_13.14_spmd} | conditional | bytes 8 | solution.py:435
  107.3 6.0 %branch_0_fun.8 = (f32[3,800,128]{2,1,0:T(8,128)}, f32[512,128]{1,0:T(8,128)}, f32[3,8,896]{2,1,0:T(8,128)}) custom-call(f32[3,800,128]{2,1,0:T(8,128)S(1)} %get-tuple-element.230.cur_ref, f32[3,800,128]{2,1,0:T(8,128)S(1)} %get-tuple-element.231.prev_ref, f32[2,800,128]{2,1,0:T(8,128)S(1)} %get-tuple-element.232.coef_ref, ...), custom_call_target="tpu_custom_call" | custom-call | tf_op jit(solution)/shard_map/cond/branch_0_fun/pallas_call | solution.py:206
  113.3 0.0 copy-start.3
  113.3 19.8 %shard_map.78 = (f32[512,128]{1,0:T(8,128)}, f32[3,104,128]{2,1,0:T(8,128)}, f32[3,104,128]{2,1,0:T(8,128)}, f32[3,8,896]{2,1,0:T(8,128)}, f32[3,8,896]{2,1,0:T(8,128)}) custom-call(f32[3,800,128]{2,1,0:T(8,128)} %get-tuple-element.328.cur_ref, f32[3,8,896]{2,1,0:T(8,128)} %get-tuple-element.329.edges_ref, f32[512,128]{1,0:T(8,128)} %get-tuple-element.330.out_ref), custom_call_target="tpu_custom_call" | custom-call | tf_op jit(solution)/shard_map/pallas_call | solution.py:349
  133.1 0.0 copy-done.3
  133.1 6.0 %conditional.9 = (f32[1,3,1,1,102400]{4,3,2,1,0:T(1,128)}) conditional(s32[]{:T(128)} %convert_element_type.14, (f32[3,800,128]{2,1,0:T(8,128)S(1)}, f32[3,800,128]{2,1,0:T(8,128)S(1)}, f32[2,800,128]{2,1,0:T(8,128)S(1)}, s32[800,128]{1,0:T(8,128)}, f32[3,104,128]{2,1,0:T(8,128)}, /*index=5*/f32[3,104,128]{2,1,0:T(8,128)}, ...), branch_computations={%region_14.15_spmd, %region_15.16_spmd} | conditional | bytes 8 | solution.py:435
  133.1 6.0 %branch_0_fun.9 = (f32[3,800,128]{2,1,0:T(8,128)}, f32[512,128]{1,0:T(8,128)}, f32[3,8,896]{2,1,0:T(8,128)}) custom-call(f32[3,800,128]{2,1,0:T(8,128)S(1)} %get-tuple-element.251.cur_ref, f32[3,800,128]{2,1,0:T(8,128)S(1)} %get-tuple-element.252.prev_ref, f32[2,800,128]{2,1,0:T(8,128)S(1)} %get-tuple-element.253.coef_ref, ...), custom_call_target="tpu_custom_call" | custom-call | tf_op jit(solution)/shard_map/cond/branch_0_fun/pallas_call | solution.py:206
  (6 shorter events, 0.1 us)
Async XLA Ops:
  0.0 31.1 %copy-start = (f32[1,3,1,1,102400]{4,3,2,1,0:T(1,128)S(1)}, f32[1,3,1,1,102400]{4,3,2,1,0:T(1,128)}, u32[]{:S(2)}) copy-start(f32[1,3,1,1,102400]{4,3,2,1,0:T(1,128)} %param.17) | copy-start | bytes 3686404
  5.6 23.3 %all-to-all-start = ((s32[128,1,4]{2,1,0:T(1,128)}), s32[128,1,4]{2,1,0:T(1,128)S(1)}, u32[]{:S(2)}, u32[]{:S(2)}) async-start(s32[128,1,4]{2,1,0:T(1,128)} %bitcast.18), calls=%async_computation | async-start | bytes 131072 | tf_op jit(solution)/shard_map/all_to_all | solution.py:374
  30.3 24.5 %collective-permute-start = (s32[512]{0:T(512)S(1)}, s32[512]{0:T(512)S(1)}, u32[]{:S(2)}, u32[]{:S(2)}) collective-permute-start(s32[512]{0:T(512)S(1)} %reshape.71), channel_id=1, source_target_pairs={{0,128},{128,0},{1,129},{129,1},{2,130},{130,2},{3,131},{131,3},{4... | collective-permute-start | bytes 6152 | tf_op jit(solution)/shard_map/ppermute | solution.py:27
  34.0 20.8 %copy-start.1 = (f32[1,2,1,1,102400]{4,3,2,1,0:T(1,128)S(1)}, f32[1,2,1,1,102400]{4,3,2,1,0:T(1,128)}, u32[]{:S(2)}) copy-start(f32[1,2,1,1,102400]{4,3,2,1,0:T(1,128)} %param.19) | copy-start | bytes 2457604
  87.3 20.0 %copy-start.2 = (f32[3,800,128]{2,1,0:T(8,128)S(1)}, f32[3,800,128]{2,1,0:T(8,128)}, u32[]{:S(2)}) copy-start(f32[3,800,128]{2,1,0:T(8,128)} %get-tuple-element.320.cur_ref) | copy-start | bytes 3686404
  113.3 19.9 %copy-start.3 = (f32[3,800,128]{2,1,0:T(8,128)S(1)}, f32[3,800,128]{2,1,0:T(8,128)}, u32[]{:S(2)}) copy-start(f32[3,800,128]{2,1,0:T(8,128)} %get-tuple-element.328.cur_ref) | copy-start | bytes 3686404
where the time goes:
time: 140 us; the launch traced here: 139 us
  Pallas kernels  108 us (77%)
  starting transfers between devices  16.7 us (12%)
  local copies, waits for them, and re-layouts  7.32 us (5%)
  waiting for transfers between devices  4.24 us (3%)
  other arithmetic  2.8 us (2%)
    pallas_call x4, Pallas kernels, exchange(): pl.pallas_call(functools.partial(exchange_kernel, (owners, rows_of, colum...  80.6 us
    pallas_call x4, Pallas kernels, run_step(): pl.pallas_call(kernel, out_shape=(jax.ShapeDtypeStruct((3, ROWS, CY), jnp...  24.2 us
    all_to_all x1, starting transfers between devices, route(): lax.all_to_all(tile_rows, ('gx', 'gy'), split_axis=0, concat_axis=0, tile...  16.1 us
    all_to_all x1, waiting for transfers between devices, route(): lax.all_to_all(tile_rows, ('gx', 'gy'), split_axis=0, concat_axis=0, tile...  4.24 us
    pallas_call x1, Pallas kernels, prepare(): pl.pallas_call(functools.partial(prepare_kernel, tiles_of), out_shape=(ja...  2.9 us
  transfers between devices with their start and end apart: 2, of which 1 were waited for; matrix products, arithmetic and copies ran while one was open for 2% of the time, Pallas kernels for 17%

commit v1 on v0

--- a/solution.py
+++ b/solution.py
@@ -362,7 +362,7 @@
             pltpu.SemaphoreType.DMA((2,)),
             pltpu.SemaphoreType.DMA((2,)),
         ],
-        compiler_params=pltpu.CompilerParams(collective_id=0, has_side_effects=True),
+        compiler_params=pltpu.CompilerParams(collective_id=outgoing.shape[1] // CY - 1, has_side_effects=True),
     )(current, edges, outgoing)
 
 
@@ -402,16 +402,20 @@
     slot_rows = jnp.full((owners * CAP,), -1, jnp.int32).at[position].set(source_rows)
     slot_weights = jnp.zeros((owners * CAP,), jnp.float32).at[position].set(weights)
     pick = jnp.where(slot_rows[:, None] == jnp.arange(fine_rows, dtype=jnp.int32)[None, :], slot_weights[:, None], 0.0)
-    arrived_rows = deliver(jnp.zeros((owners, CAP, CY), jnp.float32), send_rows)[1].reshape(1, -1)
     outgoing, edges = lax.cond(
         section == 0,
         lambda: prepare(elastic_tiles, current, pick),
         lambda: prepare(shallow_tiles, current, pick),
     )
+    row_lanes = jnp.broadcast_to(send_rows.reshape(-1, 1).astype(jnp.float32), (owners * CAP, CY))
+    outgoing = jnp.concatenate([outgoing, row_lanes], axis=1)
     for step_index in range(STEPS):
         arrived, low_x, high_x, low_y, high_y = exchange(
             current, edges, outgoing, owners, lax.axis_size("gx"), lax.axis_size("gy")
         )
+        if step_index == 0:
+            arrived_rows = arrived[:, CY].astype(jnp.int32).reshape(1, -1)
+            arrived = arrived[:, :CY]
 
         def elastic_branch():
             scratch = [

time: 140 us -> 130 us (0.929)
  starting transfers between devices: 16.7 us -> 0 us
  Pallas kernels: 108 us -> 117 us
  waiting for transfers between devices: 4.24 us -> 0 us
    all_to_all x1 -> x0, starting transfers between devices: 16.1 us -> none  [route(): lax.all_to_all(tile_rows, ('gx', 'gy'), split_axis=0, concat_axis=0, tile...]
    pallas_call x4, Pallas kernels: 80.6 us -> 90.4 us  [exchange(): pl.pallas_call(functools.partial(exchange_kernel, (owners, rows_of, colum...]
    all_to_all x1 -> x0, waiting for transfers between devices: 4.24 us -> none  [route(): lax.all_to_all(tile_rows, ('gx', 'gy'), split_axis=0, concat_axis=0, tile...]
    slice x0 -> x1, local copies, waits for them, and re-layouts: none -> 1.67 us  [on_device(): arrived = arrived[:, :CY]]
  transfers between devices with their start and end apart: 2 -> 0, of which waited for: 1 -> 0; matrix products, arithmetic and copies ran while one was open for 2% -> 0% of each run, Pallas kernels for 17% -> 0%
where the time goes in v1:
time: 130 us
  Pallas kernels  117 us (90%)
  local copies, waits for them, and re-layouts  7.76 us (6%)
  other arithmetic  3.97 us (3%)
    pallas_call x4, Pallas kernels, exchange(): pl.pallas_call(functools.partial(exchange_kernel, (owners, rows_of, colum...  90.4 us
    pallas_call x4, Pallas kernels, run_step(): pl.pallas_call(kernel, out_shape=(jax.ShapeDtypeStruct((3, ROWS, CY), jnp...  24.2 us
    pallas_call x1, Pallas kernels, prepare(): pl.pallas_call(functools.partial(prepare_kernel, tiles_of), out_shape=(ja...  2.9 us

profile of v1, /device:TPU:31, one launch (start us, length us, event | category | flops | bytes accessed | tf_op | source)
XLA Modules:
  0.0 129.6 jit_solution(4664236293679766400)
XLA Ops:
  0.0 0.0 copy-start
  0.0 0.8 fusion.12
  0.8 0.8 copy.12
  1.6 0.2 fusion.1
  1.9 0.9 fusion.3
  2.8 0.7 compare_select_fusion
  3.4 1.4 %scatter_custom_fusion.2 = s32[512]{0:T(512)S(1)} fusion(s32[256]{0:T(256)S(1)} %bitcast.71, s32[256]{0:T(256)S(1)} %bitcast.75, s32[]{:T(128)} %constant.9.clone.1), kind=kCustom, calls=%fused_computation.19 | custom fusion | bytes 2052 | tf_op jit(solution)/shard_map/scatter | solution.py:401
  4.9 1.4 %scatter_custom_fusion = s32[512]{0:T(512)S(1)} fusion(s32[256]{0:T(256)S(1)} %bitcast.72, s32[256]{0:T(256)S(1)} %bitcast.74, s32[]{:T(128)} %constant.10.clone.1), kind=kCustom, calls=%fused_computation.23 | custom fusion | bytes 2052 | tf_op jit(solution)/shard_map/scatter | solution.py:402
  6.3 1.6 %scatter_custom_fusion.1 = f32[512]{0:T(512)S(1)} fusion(s32[256]{0:T(256)S(1)} %bitcast.73, f32[256]{0:T(256)} %bitcast.78, f32[]{:T(128)} %constant.22.clone.1), kind=kCustom, calls=%fused_computation.21 | custom fusion | bytes 2560 | tf_op jit(solution)/shard_map/scatter | solution.py:403
  7.8 0.2 fusion
  8.0 0.0 copy-done
  8.0 0.1 broadcast_in_dim.38
  8.2 2.9 %conditional.5 = ((f32[512,128]{1,0:T(8,128)S(1)}, f32[3,8,896]{2,1,0:T(8,128)S(1)})) conditional(s32[]{:T(128)} %convert_element_type.31, (f32[3,800,128]{2,1,0:T(8,128)S(1)}, f32[512,80]{1,0:T(8,128)S(1)}) %tuple.67, (f32[3,800,128]{2,1,0:T(8,128)S(1)}, f32[512,80]{1,0:T(8,128)S(1)}) %tuple.68), branch_computations={%region_5.6_spmd, %region_6.7_spmd} | conditional | bytes 8 | solution.py:405
  8.2 2.9 %branch_0_fun.5 = (f32[512,128]{1,0:T(8,128)S(1)}, f32[3,8,896]{2,1,0:T(8,128)S(1)}) custom-call(f32[3,800,128]{2,1,0:T(8,128)S(1)} %get-tuple-element.184.cur_ref, f32[512,80]{1,0:T(8,128)S(1)} %get-tuple-element.185.pick_ref), custom_call_target="tpu_custom_call" | custom-call | tf_op jit(solution)/shard_map/cond/branch_0_fun/pallas_call | solution.py:189
  11.1 0.9 pad_maximum_fusion.out_ref
  11.9 0.0 copy-start.1
  11.9 29.1 %shard_map.75 = (f32[512,256]{1,0:T(8,128)}, f32[3,104,128]{2,1,0:T(8,128)}, f32[3,104,128]{2,1,0:T(8,128)}, f32[3,8,896]{2,1,0:T(8,128)}, f32[3,8,896]{2,1,0:T(8,128)}) custom-call(f32[3,800,128]{2,1,0:T(8,128)S(1)} %bitcast.37, f32[3,8,896]{2,1,0:T(8,128)S(1)} %get-tuple-element.305.edges_ref, f32[512,256]{1,0:T(8,128)} %pad_maximum_fusion.out_ref), custom_call_target="tpu_custom_call" | custom-call | tf_op jit(solution)/shard_map/pallas_call | solution.py:349
  41.1 1.1 convert_reduce_fusion
  42.2 1.7 %slice.23 = f32[512,128]{1,0:T(8,128)} slice(f32[512,256]{1,0:T(8,128)} %get-tuple-element.311), slice={[0:512], [0:128]} | slice | bytes 524288 | tf_op jit(solution)/shard_map/slice | solution.py:418
  43.9 0.0 copy-done.1
  43.9 6.3 %conditional.6 = ((f32[3,800,128]{2,1,0:T(8,128)S(1)}, f32[512,128]{1,0:T(8,128)}, f32[3,8,896]{2,1,0:T(8,128)})) conditional(s32[]{:T(128)} %convert_element_type.31, (f32[3,800,128]{2,1,0:T(8,128)S(1)}, f32[3,800,128]{2,1,0:T(8,128)}, f32[2,800,128]{2,1,0:T(8,128)S(1)}, s32[800,128]{1,0:T(8,128)}, f32[3,104,128]{2,1,0:T(8,128)}, ...), branch_computations={%region_8.9_spmd, %region_9.10_spmd} | conditional | bytes 8 | solution.py:439
  43.9 6.3 %branch_0_fun.6 = (f32[3,800,128]{2,1,0:T(8,128)S(1)}, f32[512,128]{1,0:T(8,128)}, f32[3,8,896]{2,1,0:T(8,128)}) custom-call(f32[3,800,128]{2,1,0:T(8,128)S(1)} %get-tuple-element.188.cur_ref, f32[3,800,128]{2,1,0:T(8,128)} %get-tuple-element.189.prev_ref, f32[2,800,128]{2,1,0:T(8,128)S(1)} %get-tuple-element.190.coef_ref, ...), custom_call_target="tpu_custom_call" | custom-call | tf_op jit(solution)/shard_map/cond/branch_0_fun/pallas_call | solution.py:206
  50.2 20.5 %shard_map.76 = (f32[512,128]{1,0:T(8,128)}, f32[3,104,128]{2,1,0:T(8,128)}, f32[3,104,128]{2,1,0:T(8,128)}, f32[3,8,896]{2,1,0:T(8,128)}, f32[3,8,896]{2,1,0:T(8,128)}) custom-call(f32[3,800,128]{2,1,0:T(8,128)S(1)} %get-tuple-element.312.cur_ref, f32[3,8,896]{2,1,0:T(8,128)} %get-tuple-element.313.edges_ref, f32[512,128]{1,0:T(8,128)} %get-tuple-element.314.out_ref), custom_call_target="tpu_custom_call" | custom-call | tf_op jit(solution)/shard_map/pallas_call | solution.py:349
  70.6 6.0 %conditional.7 = ((f32[3,800,128]{2,1,0:T(8,128)}, f32[512,128]{1,0:T(8,128)}, f32[3,8,896]{2,1,0:T(8,128)})) conditional(s32[]{:T(128)} %convert_element_type.31, (f32[3,800,128]{2,1,0:T(8,128)S(1)}, f32[3,800,128]{2,1,0:T(8,128)S(1)}, f32[2,800,128]{2,1,0:T(8,128)S(1)}, s32[800,128]{1,0:T(8,128)}, f32[3,104,128]{2,1,0:T(8,128)}, ...), branch_computations={%region_10.11_spmd, %region_11.12_spmd} | conditional | bytes 8 | solution.py:439
  70.7 6.0 %branch_0_fun.7 = (f32[3,800,128]{2,1,0:T(8,128)}, f32[512,128]{1,0:T(8,128)}, f32[3,8,896]{2,1,0:T(8,128)}) custom-call(f32[3,800,128]{2,1,0:T(8,128)S(1)} %get-tuple-element.209.cur_ref, f32[3,800,128]{2,1,0:T(8,128)S(1)} %get-tuple-element.210.prev_ref, f32[2,800,128]{2,1,0:T(8,128)S(1)} %get-tuple-element.211.coef_ref, ...), custom_call_target="tpu_custom_call" | custom-call | tf_op jit(solution)/shard_map/cond/branch_0_fun/pallas_call | solution.py:206
  76.6 0.0 copy-start.2
  76.6 20.4 %shard_map.77 = (f32[512,128]{1,0:T(8,128)}, f32[3,104,128]{2,1,0:T(8,128)}, f32[3,104,128]{2,1,0:T(8,128)}, f32[3,8,896]{2,1,0:T(8,128)}, f32[3,8,896]{2,1,0:T(8,128)}) custom-call(f32[3,800,128]{2,1,0:T(8,128)} %get-tuple-element.320.cur_ref, f32[3,8,896]{2,1,0:T(8,128)} %get-tuple-element.321.edges_ref, f32[512,128]{1,0:T(8,128)} %get-tuple-element.322.out_ref), custom_call_target="tpu_custom_call" | custom-call | tf_op jit(solution)/shard_map/pallas_call | solution.py:349
  97.1 0.0 copy-done.2
  97.1 6.2 %conditional.8 = ((f32[3,800,128]{2,1,0:T(8,128)}, f32[512,128]{1,0:T(8,128)}, f32[3,8,896]{2,1,0:T(8,128)})) conditional(s32[]{:T(128)} %convert_element_type.31, (f32[3,800,128]{2,1,0:T(8,128)S(1)}, f32[3,800,128]{2,1,0:T(8,128)S(1)}, f32[2,800,128]{2,1,0:T(8,128)S(1)}, s32[800,128]{1,0:T(8,128)}, f32[3,104,128]{2,1,0:T(8,128)}, ...), branch_computations={%region_12.13_spmd, %region_13.14_spmd} | conditional | bytes 8 | solution.py:439
  97.3 6.0 %branch_0_fun.8 = (f32[3,800,128]{2,1,0:T(8,128)}, f32[512,128]{1,0:T(8,128)}, f32[3,8,896]{2,1,0:T(8,128)}) custom-call(f32[3,800,128]{2,1,0:T(8,128)S(1)} %get-tuple-element.230.cur_ref, f32[3,800,128]{2,1,0:T(8,128)S(1)} %get-tuple-element.231.prev_ref, f32[2,800,128]{2,1,0:T(8,128)S(1)} %get-tuple-element.232.coef_ref, ...), custom_call_target="tpu_custom_call" | custom-call | tf_op jit(solution)/shard_map/cond/branch_0_fun/pallas_call | solution.py:206
  103.3 0.0 copy-start.3
  103.3 20.3 %shard_map.78 = (f32[512,128]{1,0:T(8,128)}, f32[3,104,128]{2,1,0:T(8,128)}, f32[3,104,128]{2,1,0:T(8,128)}, f32[3,8,896]{2,1,0:T(8,128)}, f32[3,8,896]{2,1,0:T(8,128)}) custom-call(f32[3,800,128]{2,1,0:T(8,128)} %get-tuple-element.328.cur_ref, f32[3,8,896]{2,1,0:T(8,128)} %get-tuple-element.329.edges_ref, f32[512,128]{1,0:T(8,128)} %get-tuple-element.330.out_ref), custom_call_target="tpu_custom_call" | custom-call | tf_op jit(solution)/shard_map/pallas_call | solution.py:349
  123.6 0.0 copy-done.3
  123.6 6.0 %conditional.9 = (f32[1,3,1,1,102400]{4,3,2,1,0:T(1,128)}) conditional(s32[]{:T(128)} %convert_element_type.31, (f32[3,800,128]{2,1,0:T(8,128)S(1)}, f32[3,800,128]{2,1,0:T(8,128)S(1)}, f32[2,800,128]{2,1,0:T(8,128)S(1)}, s32[800,128]{1,0:T(8,128)}, f32[3,104,128]{2,1,0:T(8,128)}, /*index=5*/f32[3,104,128]{2,1,0:T(8,128)}, ...), branch_computations={%region_14.15_spmd, %region_15.16_spmd} | conditional | bytes 8 | solution.py:439
  123.6 6.0 %branch_0_fun.9 = (f32[3,800,128]{2,1,0:T(8,128)}, f32[512,128]{1,0:T(8,128)}, f32[3,8,896]{2,1,0:T(8,128)}) custom-call(f32[3,800,128]{2,1,0:T(8,128)S(1)} %get-tuple-element.251.cur_ref, f32[3,800,128]{2,1,0:T(8,128)S(1)} %get-tuple-element.252.prev_ref, f32[2,800,128]{2,1,0:T(8,128)S(1)} %get-tuple-element.253.coef_ref, ...), custom_call_target="tpu_custom_call" | custom-call | tf_op jit(solution)/shard_map/cond/branch_0_fun/pallas_call | solution.py:206
  (7 shorter events, 0.1 us)
Async XLA Ops:
  0.0 8.0 %copy-start = (f32[1,3,1,1,102400]{4,3,2,1,0:T(1,128)S(1)}, f32[1,3,1,1,102400]{4,3,2,1,0:T(1,128)}, u32[]{:S(2)}) copy-start(f32[1,3,1,1,102400]{4,3,2,1,0:T(1,128)} %param.17) | copy-start | bytes 3686404
  11.9 31.9 %copy-start.1 = (f32[1,2,1,1,102400]{4,3,2,1,0:T(1,128)S(1)}, f32[1,2,1,1,102400]{4,3,2,1,0:T(1,128)}, u32[]{:S(2)}) copy-start(f32[1,2,1,1,102400]{4,3,2,1,0:T(1,128)} %param.19) | copy-start | bytes 2457604
  76.6 20.4 %copy-start.2 = (f32[3,800,128]{2,1,0:T(8,128)S(1)}, f32[3,800,128]{2,1,0:T(8,128)}, u32[]{:S(2)}) copy-start(f32[3,800,128]{2,1,0:T(8,128)} %get-tuple-element.320.cur_ref) | copy-start | bytes 3686404
  103.3 20.4 %copy-start.3 = (f32[3,800,128]{2,1,0:T(8,128)S(1)}, f32[3,800,128]{2,1,0:T(8,128)}, u32[]{:S(2)}) copy-start(f32[3,800,128]{2,1,0:T(8,128)} %get-tuple-element.328.cur_ref) | copy-start | bytes 3686404

commit v2 on v1

--- a/solution.py
+++ b/solution.py
@@ -231,7 +231,8 @@
     halo[...] = jnp.zeros_like(halo)
     sides[...] = jnp.zeros_like(sides)
     barrier = pltpu.get_barrier_semaphore()
-    def greet(d, carry):
+    def greet(i, carry):
+        d = (me + i) % owners
         pl.semaphore_signal(barrier, inc=1, device_id=(other, d // columns, d % columns),
                             device_id_type=pl.DeviceIdType.MESH)
         return carry
@@ -293,7 +294,8 @@
     def _():
         slab_copy(0, 1, gx - 1).start()
 
-    def send(d, carry):
+    def send(i, carry):
+        d = (me + i) % owners
         pltpu.make_async_remote_copy(
             src_ref=out_ref.at[pl.ds(d * CAP, CAP)],
             dst_ref=land.at[pl.ds(me * CAP, CAP)],

time: 130 us -> 133 us (1.023); the launches traced: 130 us -> 131 us
  Pallas kernels: 117 us -> 119 us
where the time goes in v2:
time: 133 us; the launch traced here: 131 us
  Pallas kernels  119 us (89%)
  local copies, waits for them, and re-layouts  7.76 us (6%)
  other arithmetic  3.97 us (3%)
    pallas_call x4, Pallas kernels, exchange(): pl.pallas_call(functools.partial(exchange_kernel, (owners, rows_of, colum...  91.6 us
    pallas_call x4, Pallas kernels, run_step(): pl.pallas_call(kernel, out_shape=(jax.ShapeDtypeStruct((3, ROWS, CY), jnp...  24.2 us
    pallas_call x1, Pallas kernels, prepare(): pl.pallas_call(functools.partial(prepare_kernel, tiles_of), out_shape=(ja...  2.9 us

profile of v2, /device:TPU:31, one launch (start us, length us, event | category | flops | bytes accessed | tf_op | source)
XLA Modules:
  0.0 130.8 jit_solution(10482731075039069911)
XLA Ops:
  0.0 0.0 copy-start
  0.0 0.8 fusion.12
  0.8 0.8 copy.12
  1.6 0.2 fusion.1
  1.9 0.9 fusion.3
  2.8 0.7 compare_select_fusion
  3.4 1.4 %scatter_custom_fusion.2 = s32[512]{0:T(512)S(1)} fusion(s32[256]{0:T(256)S(1)} %bitcast.71, s32[256]{0:T(256)S(1)} %bitcast.75, s32[]{:T(128)} %constant.9.clone.1), kind=kCustom, calls=%fused_computation.19 | custom fusion | bytes 2052 | tf_op jit(solution)/shard_map/scatter | solution.py:403
  4.9 1.4 %scatter_custom_fusion = s32[512]{0:T(512)S(1)} fusion(s32[256]{0:T(256)S(1)} %bitcast.72, s32[256]{0:T(256)S(1)} %bitcast.74, s32[]{:T(128)} %constant.10.clone.1), kind=kCustom, calls=%fused_computation.23 | custom fusion | bytes 2052 | tf_op jit(solution)/shard_map/scatter | solution.py:404
  6.3 1.6 %scatter_custom_fusion.1 = f32[512]{0:T(512)S(1)} fusion(s32[256]{0:T(256)S(1)} %bitcast.73, f32[256]{0:T(256)} %bitcast.78, f32[]{:T(128)} %constant.22.clone.1), kind=kCustom, calls=%fused_computation.21 | custom fusion | bytes 2560 | tf_op jit(solution)/shard_map/scatter | solution.py:405
  7.8 0.2 fusion
  8.0 0.0 copy-done
  8.0 0.1 broadcast_in_dim.38
  8.2 2.9 %conditional.5 = ((f32[512,128]{1,0:T(8,128)S(1)}, f32[3,8,896]{2,1,0:T(8,128)S(1)})) conditional(s32[]{:T(128)} %convert_element_type.31, (f32[3,800,128]{2,1,0:T(8,128)S(1)}, f32[512,80]{1,0:T(8,128)S(1)}) %tuple.67, (f32[3,800,128]{2,1,0:T(8,128)S(1)}, f32[512,80]{1,0:T(8,128)S(1)}) %tuple.68), branch_computations={%region_5.6_spmd, %region_6.7_spmd} | conditional | bytes 8 | solution.py:407
  8.2 2.9 %branch_0_fun.5 = (f32[512,128]{1,0:T(8,128)S(1)}, f32[3,8,896]{2,1,0:T(8,128)S(1)}) custom-call(f32[3,800,128]{2,1,0:T(8,128)S(1)} %get-tuple-element.184.cur_ref, f32[512,80]{1,0:T(8,128)S(1)} %get-tuple-element.185.pick_ref), custom_call_target="tpu_custom_call" | custom-call | tf_op jit(solution)/shard_map/cond/branch_0_fun/pallas_call | solution.py:189
  11.1 0.9 pad_maximum_fusion.out_ref
  11.9 0.0 copy-start.1
  11.9 28.6 %shard_map.75 = (f32[512,256]{1,0:T(8,128)}, f32[3,104,128]{2,1,0:T(8,128)}, f32[3,104,128]{2,1,0:T(8,128)}, f32[3,8,896]{2,1,0:T(8,128)}, f32[3,8,896]{2,1,0:T(8,128)}) custom-call(f32[3,800,128]{2,1,0:T(8,128)S(1)} %bitcast.37, f32[3,8,896]{2,1,0:T(8,128)S(1)} %get-tuple-element.305.edges_ref, f32[512,256]{1,0:T(8,128)} %pad_maximum_fusion.out_ref), custom_call_target="tpu_custom_call" | custom-call | tf_op jit(solution)/shard_map/pallas_call | solution.py:351
  40.6 1.1 convert_reduce_fusion
  41.7 1.7 %slice.23 = f32[512,128]{1,0:T(8,128)} slice(f32[512,256]{1,0:T(8,128)} %get-tuple-element.311), slice={[0:512], [0:128]} | slice | bytes 524288 | tf_op jit(solution)/shard_map/slice | solution.py:420
  43.4 0.0 copy-done.1
  43.4 6.3 %conditional.6 = ((f32[3,800,128]{2,1,0:T(8,128)S(1)}, f32[512,128]{1,0:T(8,128)}, f32[3,8,896]{2,1,0:T(8,128)})) conditional(s32[]{:T(128)} %convert_element_type.31, (f32[3,800,128]{2,1,0:T(8,128)S(1)}, f32[3,800,128]{2,1,0:T(8,128)}, f32[2,800,128]{2,1,0:T(8,128)S(1)}, s32[800,128]{1,0:T(8,128)}, f32[3,104,128]{2,1,0:T(8,128)}, ...), branch_computations={%region_8.9_spmd, %region_9.10_spmd} | conditional | bytes 8 | solution.py:441
  43.4 6.3 %branch_0_fun.6 = (f32[3,800,128]{2,1,0:T(8,128)S(1)}, f32[512,128]{1,0:T(8,128)}, f32[3,8,896]{2,1,0:T(8,128)}) custom-call(f32[3,800,128]{2,1,0:T(8,128)S(1)} %get-tuple-element.188.cur_ref, f32[3,800,128]{2,1,0:T(8,128)} %get-tuple-element.189.prev_ref, f32[2,800,128]{2,1,0:T(8,128)S(1)} %get-tuple-element.190.coef_ref, ...), custom_call_target="tpu_custom_call" | custom-call | tf_op jit(solution)/shard_map/cond/branch_0_fun/pallas_call | solution.py:206
  49.7 21.0 %shard_map.76 = (f32[512,128]{1,0:T(8,128)}, f32[3,104,128]{2,1,0:T(8,128)}, f32[3,104,128]{2,1,0:T(8,128)}, f32[3,8,896]{2,1,0:T(8,128)}, f32[3,8,896]{2,1,0:T(8,128)}) custom-call(f32[3,800,128]{2,1,0:T(8,128)S(1)} %get-tuple-element.312.cur_ref, f32[3,8,896]{2,1,0:T(8,128)} %get-tuple-element.313.edges_ref, f32[512,128]{1,0:T(8,128)} %get-tuple-element.314.out_ref), custom_call_target="tpu_custom_call" | custom-call | tf_op jit(solution)/shard_map/pallas_call | solution.py:351
  70.7 6.0 %conditional.7 = ((f32[3,800,128]{2,1,0:T(8,128)}, f32[512,128]{1,0:T(8,128)}, f32[3,8,896]{2,1,0:T(8,128)})) conditional(s32[]{:T(128)} %convert_element_type.31, (f32[3,800,128]{2,1,0:T(8,128)S(1)}, f32[3,800,128]{2,1,0:T(8,128)S(1)}, f32[2,800,128]{2,1,0:T(8,128)S(1)}, s32[800,128]{1,0:T(8,128)}, f32[3,104,128]{2,1,0:T(8,128)}, ...), branch_computations={%region_10.11_spmd, %region_11.12_spmd} | conditional | bytes 8 | solution.py:441
  70.7 6.0 %branch_0_fun.7 = (f32[3,800,128]{2,1,0:T(8,128)}, f32[512,128]{1,0:T(8,128)}, f32[3,8,896]{2,1,0:T(8,128)}) custom-call(f32[3,800,128]{2,1,0:T(8,128)S(1)} %get-tuple-element.209.cur_ref, f32[3,800,128]{2,1,0:T(8,128)S(1)} %get-tuple-element.210.prev_ref, f32[2,800,128]{2,1,0:T(8,128)S(1)} %get-tuple-element.211.coef_ref, ...), custom_call_target="tpu_custom_call" | custom-call | tf_op jit(solution)/shard_map/cond/branch_0_fun/pallas_call | solution.py:206
  76.7 0.0 copy-start.2
  76.7 20.5 %shard_map.77 = (f32[512,128]{1,0:T(8,128)}, f32[3,104,128]{2,1,0:T(8,128)}, f32[3,104,128]{2,1,0:T(8,128)}, f32[3,8,896]{2,1,0:T(8,128)}, f32[3,8,896]{2,1,0:T(8,128)}) custom-call(f32[3,800,128]{2,1,0:T(8,128)} %get-tuple-element.320.cur_ref, f32[3,8,896]{2,1,0:T(8,128)} %get-tuple-element.321.edges_ref, f32[512,128]{1,0:T(8,128)} %get-tuple-element.322.out_ref), custom_call_target="tpu_custom_call" | custom-call | tf_op jit(solution)/shard_map/pallas_call | solution.py:351
  97.2 0.0 copy-done.2
  97.2 6.2 %conditional.8 = ((f32[3,800,128]{2,1,0:T(8,128)}, f32[512,128]{1,0:T(8,128)}, f32[3,8,896]{2,1,0:T(8,128)})) conditional(s32[]{:T(128)} %convert_element_type.31, (f32[3,800,128]{2,1,0:T(8,128)S(1)}, f32[3,800,128]{2,1,0:T(8,128)S(1)}, f32[2,800,128]{2,1,0:T(8,128)S(1)}, s32[800,128]{1,0:T(8,128)}, f32[3,104,128]{2,1,0:T(8,128)}, ...), branch_computations={%region_12.13_spmd, %region_13.14_spmd} | conditional | bytes 8 | solution.py:441
  97.4 6.0 %branch_0_fun.8 = (f32[3,800,128]{2,1,0:T(8,128)}, f32[512,128]{1,0:T(8,128)}, f32[3,8,896]{2,1,0:T(8,128)}) custom-call(f32[3,800,128]{2,1,0:T(8,128)S(1)} %get-tuple-element.230.cur_ref, f32[3,800,128]{2,1,0:T(8,128)S(1)} %get-tuple-element.231.prev_ref, f32[2,800,128]{2,1,0:T(8,128)S(1)} %get-tuple-element.232.coef_ref, ...), custom_call_target="tpu_custom_call" | custom-call | tf_op jit(solution)/shard_map/cond/branch_0_fun/pallas_call | solution.py:206
  103.4 0.0 copy-start.3
  103.4 21.4 %shard_map.78 = (f32[512,128]{1,0:T(8,128)}, f32[3,104,128]{2,1,0:T(8,128)}, f32[3,104,128]{2,1,0:T(8,128)}, f32[3,8,896]{2,1,0:T(8,128)}, f32[3,8,896]{2,1,0:T(8,128)}) custom-call(f32[3,800,128]{2,1,0:T(8,128)} %get-tuple-element.328.cur_ref, f32[3,8,896]{2,1,0:T(8,128)} %get-tuple-element.329.edges_ref, f32[512,128]{1,0:T(8,128)} %get-tuple-element.330.out_ref), custom_call_target="tpu_custom_call" | custom-call | tf_op jit(solution)/shard_map/pallas_call | solution.py:351
  124.8 0.0 copy-done.3
  124.8 6.0 %conditional.9 = (f32[1,3,1,1,102400]{4,3,2,1,0:T(1,128)}) conditional(s32[]{:T(128)} %convert_element_type.31, (f32[3,800,128]{2,1,0:T(8,128)S(1)}, f32[3,800,128]{2,1,0:T(8,128)S(1)}, f32[2,800,128]{2,1,0:T(8,128)S(1)}, s32[800,128]{1,0:T(8,128)}, f32[3,104,128]{2,1,0:T(8,128)}, /*index=5*/f32[3,104,128]{2,1,0:T(8,128)}, ...), branch_computations={%region_14.15_spmd, %region_15.16_spmd} | conditional | bytes 8 | solution.py:441
  124.8 6.0 %branch_0_fun.9 = (f32[3,800,128]{2,1,0:T(8,128)}, f32[512,128]{1,0:T(8,128)}, f32[3,8,896]{2,1,0:T(8,128)}) custom-call(f32[3,800,128]{2,1,0:T(8,128)S(1)} %get-tuple-element.251.cur_ref, f32[3,800,128]{2,1,0:T(8,128)S(1)} %get-tuple-element.252.prev_ref, f32[2,800,128]{2,1,0:T(8,128)S(1)} %get-tuple-element.253.coef_ref, ...), custom_call_target="tpu_custom_call" | custom-call | tf_op jit(solution)/shard_map/cond/branch_0_fun/pallas_call | solution.py:206
  (7 shorter events, 0.1 us)
Async XLA Ops:
  0.0 8.0 %copy-start = (f32[1,3,1,1,102400]{4,3,2,1,0:T(1,128)S(1)}, f32[1,3,1,1,102400]{4,3,2,1,0:T(1,128)}, u32[]{:S(2)}) copy-start(f32[1,3,1,1,102400]{4,3,2,1,0:T(1,128)} %param.17) | copy-start | bytes 3686404
  11.9 31.4 %copy-start.1 = (f32[1,2,1,1,102400]{4,3,2,1,0:T(1,128)S(1)}, f32[1,2,1,1,102400]{4,3,2,1,0:T(1,128)}, u32[]{:S(2)}) copy-start(f32[1,2,1,1,102400]{4,3,2,1,0:T(1,128)} %param.19) | copy-start | bytes 2457604
  76.7 20.5 %copy-start.2 = (f32[3,800,128]{2,1,0:T(8,128)S(1)}, f32[3,800,128]{2,1,0:T(8,128)}, u32[]{:S(2)}) copy-start(f32[3,800,128]{2,1,0:T(8,128)} %get-tuple-element.320.cur_ref) | copy-start | bytes 3686404
  103.4 21.4 %copy-start.3 = (f32[3,800,128]{2,1,0:T(8,128)S(1)}, f32[3,800,128]{2,1,0:T(8,128)}, u32[]{:S(2)}) copy-start(f32[3,800,128]{2,1,0:T(8,128)} %get-tuple-element.328.cur_ref) | copy-start | bytes 3686404

commit v3 on v1

--- a/solution.py
+++ b/solution.py
@@ -65,7 +65,7 @@
 def landing_sum(rows_ref, arrived_ref, count):
     slots = rows_ref.shape[1]
     one_hot = (lax.broadcasted_iota(jnp.int32, (count, slots), 0) == rows_ref[...]).astype(jnp.float32)
-    return exact_dot(one_hot, arrived_ref[...])
+    return select_dot(one_hot, arrived_ref[...])
 
 
 def edge_rows(out_ref, edges_ref):

time: 130 us -> 130 us (level)
  no operation moved by 1% of the time
where the time goes in v3:
time: 130 us; the launch traced here: 129 us
  Pallas kernels  117 us (90%)
  local copies, waits for them, and re-layouts  7.76 us (6%)
  other arithmetic  3.97 us (3%)
    pallas_call x4, Pallas kernels, exchange(): pl.pallas_call(functools.partial(exchange_kernel, (owners, rows_of, colum...  90.4 us
    pallas_call x4, Pallas kernels, run_step(): pl.pallas_call(kernel, out_shape=(jax.ShapeDtypeStruct((3, ROWS, CY), jnp...  24 us
    pallas_call x1, Pallas kernels, prepare(): pl.pallas_call(functools.partial(prepare_kernel, tiles_of), out_shape=(ja...  2.9 us

profile of v3, /device:TPU:31, one launch (start us, length us, event | category | flops | bytes accessed | tf_op | source)
XLA Modules:
  0.0 129.4 jit_solution(9718875599136719694)
XLA Ops:
  0.0 0.0 copy-start
  0.0 0.8 fusion.12
  0.8 0.8 copy.12
  1.6 0.2 fusion.1
  1.9 0.9 fusion.3
  2.8 0.7 compare_select_fusion
  3.4 1.4 %scatter_custom_fusion.2 = s32[512]{0:T(512)S(1)} fusion(s32[256]{0:T(256)S(1)} %bitcast.71, s32[256]{0:T(256)S(1)} %bitcast.75, s32[]{:T(128)} %constant.9.clone.1), kind=kCustom, calls=%fused_computation.19 | custom fusion | bytes 2052 | tf_op jit(solution)/shard_map/scatter | solution.py:401
  4.9 1.4 %scatter_custom_fusion = s32[512]{0:T(512)S(1)} fusion(s32[256]{0:T(256)S(1)} %bitcast.72, s32[256]{0:T(256)S(1)} %bitcast.74, s32[]{:T(128)} %constant.10.clone.1), kind=kCustom, calls=%fused_computation.23 | custom fusion | bytes 2052 | tf_op jit(solution)/shard_map/scatter | solution.py:402
  6.3 1.6 %scatter_custom_fusion.1 = f32[512]{0:T(512)S(1)} fusion(s32[256]{0:T(256)S(1)} %bitcast.73, f32[256]{0:T(256)} %bitcast.78, f32[]{:T(128)} %constant.22.clone.1), kind=kCustom, calls=%fused_computation.21 | custom fusion | bytes 2560 | tf_op jit(solution)/shard_map/scatter | solution.py:403
  7.8 0.2 fusion
  8.0 0.0 copy-done
  8.0 0.1 broadcast_in_dim.38
  8.2 2.9 %conditional.5 = ((f32[512,128]{1,0:T(8,128)S(1)}, f32[3,8,896]{2,1,0:T(8,128)S(1)})) conditional(s32[]{:T(128)} %convert_element_type.31, (f32[3,800,128]{2,1,0:T(8,128)S(1)}, f32[512,80]{1,0:T(8,128)S(1)}) %tuple.67, (f32[3,800,128]{2,1,0:T(8,128)S(1)}, f32[512,80]{1,0:T(8,128)S(1)}) %tuple.68), branch_computations={%region_5.6_spmd, %region_6.7_spmd} | conditional | bytes 8 | solution.py:405
  8.2 2.9 %branch_0_fun.5 = (f32[512,128]{1,0:T(8,128)S(1)}, f32[3,8,896]{2,1,0:T(8,128)S(1)}) custom-call(f32[3,800,128]{2,1,0:T(8,128)S(1)} %get-tuple-element.184.cur_ref, f32[512,80]{1,0:T(8,128)S(1)} %get-tuple-element.185.pick_ref), custom_call_target="tpu_custom_call" | custom-call | tf_op jit(solution)/shard_map/cond/branch_0_fun/pallas_call | solution.py:189
  11.1 0.9 pad_maximum_fusion.out_ref
  11.9 0.0 copy-start.1
  11.9 29.1 %shard_map.75 = (f32[512,256]{1,0:T(8,128)}, f32[3,104,128]{2,1,0:T(8,128)}, f32[3,104,128]{2,1,0:T(8,128)}, f32[3,8,896]{2,1,0:T(8,128)}, f32[3,8,896]{2,1,0:T(8,128)}) custom-call(f32[3,800,128]{2,1,0:T(8,128)S(1)} %bitcast.37, f32[3,8,896]{2,1,0:T(8,128)S(1)} %get-tuple-element.305.edges_ref, f32[512,256]{1,0:T(8,128)} %pad_maximum_fusion.out_ref), custom_call_target="tpu_custom_call" | custom-call | tf_op jit(solution)/shard_map/pallas_call | solution.py:349
  41.1 1.1 convert_reduce_fusion
  42.2 1.7 %slice.23 = f32[512,128]{1,0:T(8,128)} slice(f32[512,256]{1,0:T(8,128)} %get-tuple-element.311), slice={[0:512], [0:128]} | slice | bytes 524288 | tf_op jit(solution)/shard_map/slice | solution.py:418
  43.9 0.0 copy-done.1
  43.9 6.3 %conditional.6 = ((f32[3,800,128]{2,1,0:T(8,128)S(1)}, f32[512,128]{1,0:T(8,128)}, f32[3,8,896]{2,1,0:T(8,128)})) conditional(s32[]{:T(128)} %convert_element_type.31, (f32[3,800,128]{2,1,0:T(8,128)S(1)}, f32[3,800,128]{2,1,0:T(8,128)}, f32[2,800,128]{2,1,0:T(8,128)S(1)}, s32[800,128]{1,0:T(8,128)}, f32[3,104,128]{2,1,0:T(8,128)}, ...), branch_computations={%region_8.9_spmd, %region_9.10_spmd} | conditional | bytes 8 | solution.py:439
  43.9 6.3 %branch_0_fun.6 = (f32[3,800,128]{2,1,0:T(8,128)S(1)}, f32[512,128]{1,0:T(8,128)}, f32[3,8,896]{2,1,0:T(8,128)}) custom-call(f32[3,800,128]{2,1,0:T(8,128)S(1)} %get-tuple-element.188.cur_ref, f32[3,800,128]{2,1,0:T(8,128)} %get-tuple-element.189.prev_ref, f32[2,800,128]{2,1,0:T(8,128)S(1)} %get-tuple-element.190.coef_ref, ...), custom_call_target="tpu_custom_call" | custom-call | tf_op jit(solution)/shard_map/cond/branch_0_fun/pallas_call | solution.py:206
  50.1 20.5 %shard_map.76 = (f32[512,128]{1,0:T(8,128)}, f32[3,104,128]{2,1,0:T(8,128)}, f32[3,104,128]{2,1,0:T(8,128)}, f32[3,8,896]{2,1,0:T(8,128)}, f32[3,8,896]{2,1,0:T(8,128)}) custom-call(f32[3,800,128]{2,1,0:T(8,128)S(1)} %get-tuple-element.312.cur_ref, f32[3,8,896]{2,1,0:T(8,128)} %get-tuple-element.313.edges_ref, f32[512,128]{1,0:T(8,128)} %get-tuple-element.314.out_ref), custom_call_target="tpu_custom_call" | custom-call | tf_op jit(solution)/shard_map/pallas_call | solution.py:349
  70.6 5.9 %conditional.7 = ((f32[3,800,128]{2,1,0:T(8,128)}, f32[512,128]{1,0:T(8,128)}, f32[3,8,896]{2,1,0:T(8,128)})) conditional(s32[]{:T(128)} %convert_element_type.31, (f32[3,800,128]{2,1,0:T(8,128)S(1)}, f32[3,800,128]{2,1,0:T(8,128)S(1)}, f32[2,800,128]{2,1,0:T(8,128)S(1)}, s32[800,128]{1,0:T(8,128)}, f32[3,104,128]{2,1,0:T(8,128)}, ...), branch_computations={%region_10.11_spmd, %region_11.12_spmd} | conditional | bytes 8 | solution.py:439
  70.6 5.9 %branch_0_fun.7 = (f32[3,800,128]{2,1,0:T(8,128)}, f32[512,128]{1,0:T(8,128)}, f32[3,8,896]{2,1,0:T(8,128)}) custom-call(f32[3,800,128]{2,1,0:T(8,128)S(1)} %get-tuple-element.209.cur_ref, f32[3,800,128]{2,1,0:T(8,128)S(1)} %get-tuple-element.210.prev_ref, f32[2,800,128]{2,1,0:T(8,128)S(1)} %get-tuple-element.211.coef_ref, ...), custom_call_target="tpu_custom_call" | custom-call | tf_op jit(solution)/shard_map/cond/branch_0_fun/pallas_call | solution.py:206
  76.5 0.0 copy-start.2
  76.5 20.4 %shard_map.77 = (f32[512,128]{1,0:T(8,128)}, f32[3,104,128]{2,1,0:T(8,128)}, f32[3,104,128]{2,1,0:T(8,128)}, f32[3,8,896]{2,1,0:T(8,128)}, f32[3,8,896]{2,1,0:T(8,128)}) custom-call(f32[3,800,128]{2,1,0:T(8,128)} %get-tuple-element.320.cur_ref, f32[3,8,896]{2,1,0:T(8,128)} %get-tuple-element.321.edges_ref, f32[512,128]{1,0:T(8,128)} %get-tuple-element.322.out_ref), custom_call_target="tpu_custom_call" | custom-call | tf_op jit(solution)/shard_map/pallas_call | solution.py:349
  97.0 0.0 copy-done.2
  97.0 6.2 %conditional.8 = ((f32[3,800,128]{2,1,0:T(8,128)}, f32[512,128]{1,0:T(8,128)}, f32[3,8,896]{2,1,0:T(8,128)})) conditional(s32[]{:T(128)} %convert_element_type.31, (f32[3,800,128]{2,1,0:T(8,128)S(1)}, f32[3,800,128]{2,1,0:T(8,128)S(1)}, f32[2,800,128]{2,1,0:T(8,128)S(1)}, s32[800,128]{1,0:T(8,128)}, f32[3,104,128]{2,1,0:T(8,128)}, ...), branch_computations={%region_12.13_spmd, %region_13.14_spmd} | conditional | bytes 8 | solution.py:439
  97.2 5.9 %branch_0_fun.8 = (f32[3,800,128]{2,1,0:T(8,128)}, f32[512,128]{1,0:T(8,128)}, f32[3,8,896]{2,1,0:T(8,128)}) custom-call(f32[3,800,128]{2,1,0:T(8,128)S(1)} %get-tuple-element.230.cur_ref, f32[3,800,128]{2,1,0:T(8,128)S(1)} %get-tuple-element.231.prev_ref, f32[2,800,128]{2,1,0:T(8,128)S(1)} %get-tuple-element.232.coef_ref, ...), custom_call_target="tpu_custom_call" | custom-call | tf_op jit(solution)/shard_map/cond/branch_0_fun/pallas_call | solution.py:206
  103.1 0.0 copy-start.3
  103.1 20.3 %shard_map.78 = (f32[512,128]{1,0:T(8,128)}, f32[3,104,128]{2,1,0:T(8,128)}, f32[3,104,128]{2,1,0:T(8,128)}, f32[3,8,896]{2,1,0:T(8,128)}, f32[3,8,896]{2,1,0:T(8,128)}) custom-call(f32[3,800,128]{2,1,0:T(8,128)} %get-tuple-element.328.cur_ref, f32[3,8,896]{2,1,0:T(8,128)} %get-tuple-element.329.edges_ref, f32[512,128]{1,0:T(8,128)} %get-tuple-element.330.out_ref), custom_call_target="tpu_custom_call" | custom-call | tf_op jit(solution)/shard_map/pallas_call | solution.py:349
  123.5 0.0 copy-done.3
  123.5 5.9 %conditional.9 = (f32[1,3,1,1,102400]{4,3,2,1,0:T(1,128)}) conditional(s32[]{:T(128)} %convert_element_type.31, (f32[3,800,128]{2,1,0:T(8,128)S(1)}, f32[3,800,128]{2,1,0:T(8,128)S(1)}, f32[2,800,128]{2,1,0:T(8,128)S(1)}, s32[800,128]{1,0:T(8,128)}, f32[3,104,128]{2,1,0:T(8,128)}, /*index=5*/f32[3,104,128]{2,1,0:T(8,128)}, ...), branch_computations={%region_14.15_spmd, %region_15.16_spmd} | conditional | bytes 8 | solution.py:439
  123.5 5.9 %branch_0_fun.9 = (f32[3,800,128]{2,1,0:T(8,128)}, f32[512,128]{1,0:T(8,128)}, f32[3,8,896]{2,1,0:T(8,128)}) custom-call(f32[3,800,128]{2,1,0:T(8,128)S(1)} %get-tuple-element.251.cur_ref, f32[3,800,128]{2,1,0:T(8,128)S(1)} %get-tuple-element.252.prev_ref, f32[2,800,128]{2,1,0:T(8,128)S(1)} %get-tuple-element.253.coef_ref, ...), custom_call_target="tpu_custom_call" | custom-call | tf_op jit(solution)/shard_map/cond/branch_0_fun/pallas_call | solution.py:206
  (7 shorter events, 0.1 us)
Async XLA Ops:
  0.0 8.0 %copy-start = (f32[1,3,1,1,102400]{4,3,2,1,0:T(1,128)S(1)}, f32[1,3,1,1,102400]{4,3,2,1,0:T(1,128)}, u32[]{:S(2)}) copy-start(f32[1,3,1,1,102400]{4,3,2,1,0:T(1,128)} %param.17) | copy-start | bytes 3686404
  11.9 31.9 %copy-start.1 = (f32[1,2,1,1,102400]{4,3,2,1,0:T(1,128)S(1)}, f32[1,2,1,1,102400]{4,3,2,1,0:T(1,128)}, u32[]{:S(2)}) copy-start(f32[1,2,1,1,102400]{4,3,2,1,0:T(1,128)} %param.19) | copy-start | bytes 2457604
  76.5 20.4 %copy-start.2 = (f32[3,800,128]{2,1,0:T(8,128)S(1)}, f32[3,800,128]{2,1,0:T(8,128)}, u32[]{:S(2)}) copy-start(f32[3,800,128]{2,1,0:T(8,128)} %get-tuple-element.320.cur_ref) | copy-start | bytes 3686404
  103.1 20.4 %copy-start.3 = (f32[3,800,128]{2,1,0:T(8,128)S(1)}, f32[3,800,128]{2,1,0:T(8,128)}, u32[]{:S(2)}) copy-start(f32[3,800,128]{2,1,0:T(8,128)} %get-tuple-element.328.cur_ref) | copy-start | bytes 3686404

commit v4 on v1

--- a/solution.py
+++ b/solution.py
@@ -125,13 +125,23 @@
     edge_rows(out_ref, edges_ref)
 
 
-def shallow_kernel(cur_ref, prev_ref, coef_ref, wet_ref, low_ref, high_ref, low_rows_ref, high_rows_ref, rows_ref,
-                   arrived_ref, pick_ref, out_ref, tiles_ref, edges_ref, scratch, source_ref, left_pad, right_pad):
+def shallow_kernel(cur_ref, prev_hbm, coef_hbm, wet_hbm, low_ref, high_ref, low_rows_ref, high_rows_ref, rows_ref,
+                   arrived_ref, pick_ref, out_ref, tiles_ref, edges_ref, scratch, source_ref, left_pad, right_pad,
+                   prev_ref, coef_ref, wet_ref, load_sem):
+    loads = [
+        pltpu.make_async_copy(prev_hbm, prev_ref, load_sem.at[0]),
+        pltpu.make_async_copy(coef_hbm, coef_ref, load_sem.at[1]),
+        pltpu.make_async_copy(wet_hbm, wet_ref, load_sem.at[2]),
+    ]
+    for load in loads:
+        load.start()
     fill_scratch(scratch, cur_ref, low_ref, high_ref, 3)
     fill_sides(low_rows_ref, high_rows_ref, left_pad, right_pad)
     coarse_source = landing_sum(rows_ref, arrived_ref, REFINE * CX)
     for cb in range(REFINE):
         source_ref[pl.ds(cb, REFINE * CX, stride=REFINE), :] = select_dot(coarse_source, spread(cb))
+    for load in loads:
+        load.wait()
     lanes = lane_index(CHUNK)
     first_lane = lanes == 0
     last_lane = lanes == CY - 1
@@ -201,8 +211,10 @@
     return [pl.BlockSpec(memory_space=pltpu.VMEM)] * count
 
 
-def run_step(kernel, scratch_shapes, *operands):
+def run_step(kernel, scratch_shapes, *operands, in_hbm=()):
     slots = operands[-1].shape[0]
+    specs = [pl.BlockSpec(memory_space=pl.ANY) if i in in_hbm else pl.BlockSpec(memory_space=pltpu.VMEM)
+             for i in range(len(operands))]
     return pl.pallas_call(
         kernel,
         out_shape=(
@@ -210,7 +222,7 @@
             jax.ShapeDtypeStruct((slots, CY), jnp.float32),
             jax.ShapeDtypeStruct((3, 8, EDGE_LANES), jnp.float32),
         ),
-        in_specs=vmem_specs(len(operands)),
+        in_specs=specs,
         out_specs=tuple(vmem_specs(3)),
         scratch_shapes=scratch_shapes,
     )(*operands)
@@ -432,9 +444,13 @@
                 pltpu.VMEM((ROWS, CY), jnp.float32),
                 pltpu.VMEM((3, ROWS + 2 * EDGE, 1), jnp.float32),
                 pltpu.VMEM((3, ROWS + 2 * EDGE, 1), jnp.float32),
+                pltpu.VMEM((3, ROWS, CY), jnp.float32),
+                pltpu.VMEM((2, ROWS, CY), jnp.float32),
+                pltpu.VMEM((ROWS, CY), jnp.int32),
+                pltpu.SemaphoreType.DMA((3,)),
             ]
             return run_step(shallow_kernel, scratch, current, earlier, factors, wet, low_x, high_x, low_y, high_y,
-                            arrived_rows, arrived, pick)
+                            arrived_rows, arrived, pick, in_hbm=(1, 2, 3))
 
         updated, outgoing, edges = lax.cond(section == 0, elastic_branch, shallow_branch)
         earlier, current = (current, updated)

time: 130 us -> 135 us (1.038)
  Pallas kernels: 117 us -> 121 us
    pallas_call x4, Pallas kernels: 24.2 us -> 27.8 us  [run_step(): pl.pallas_call(kernel, out_shape=(jax.ShapeDtypeStruct((3, ROWS, CY), jnp...]
where the time goes in v4:
time: 135 us; the launch traced here: 134 us
  Pallas kernels  121 us (90%)
  local copies, waits for them, and re-layouts  7.76 us (6%)
  other arithmetic  3.97 us (3%)
    pallas_call x4, Pallas kernels, exchange(): pl.pallas_call(functools.partial(exchange_kernel, (owners, rows_of, colum...  90.8 us
    pallas_call x4, Pallas kernels, run_step(): pl.pallas_call(kernel, out_shape=(jax.ShapeDtypeStruct((3, ROWS, CY), jnp...  27.8 us
    pallas_call x1, Pallas kernels, prepare(): pl.pallas_call(functools.partial(prepare_kernel, tiles_of), out_shape=(ja...  2.9 us

profile of v4, /device:TPU:31, one launch (start us, length us, event | category | flops | bytes accessed | tf_op | source)
XLA Modules:
  0.0 134.1 jit_solution(15047403341774874238)
XLA Ops:
  0.0 0.0 copy-start
  0.0 0.8 fusion.12
  0.8 0.8 copy.12
  1.6 0.2 fusion.1
  1.9 0.9 fusion.3
  2.8 0.7 compare_select_fusion
  3.4 1.4 %scatter_custom_fusion.2 = s32[512]{0:T(512)S(1)} fusion(s32[256]{0:T(256)S(1)} %bitcast.71, s32[256]{0:T(256)S(1)} %bitcast.75, s32[]{:T(128)} %constant.9.clone.1), kind=kCustom, calls=%fused_computation.19 | custom fusion | bytes 2052 | tf_op jit(solution)/shard_map/scatter | solution.py:413
  4.9 1.4 %scatter_custom_fusion = s32[512]{0:T(512)S(1)} fusion(s32[256]{0:T(256)S(1)} %bitcast.72, s32[256]{0:T(256)S(1)} %bitcast.74, s32[]{:T(128)} %constant.10.clone.1), kind=kCustom, calls=%fused_computation.23 | custom fusion | bytes 2052 | tf_op jit(solution)/shard_map/scatter | solution.py:414
  6.3 1.6 %scatter_custom_fusion.1 = f32[512]{0:T(512)S(1)} fusion(s32[256]{0:T(256)S(1)} %bitcast.73, f32[256]{0:T(256)} %bitcast.78, f32[]{:T(128)} %constant.22.clone.1), kind=kCustom, calls=%fused_computation.21 | custom fusion | bytes 2560 | tf_op jit(solution)/shard_map/scatter | solution.py:415
  7.8 0.2 fusion
  8.0 0.0 copy-done
  8.0 0.1 broadcast_in_dim.38
  8.2 2.9 %conditional.5 = ((f32[512,128]{1,0:T(8,128)S(1)}, f32[3,8,896]{2,1,0:T(8,128)S(1)})) conditional(s32[]{:T(128)} %convert_element_type.31, (f32[3,800,128]{2,1,0:T(8,128)S(1)}, f32[512,80]{1,0:T(8,128)S(1)}) %tuple.67, (f32[3,800,128]{2,1,0:T(8,128)S(1)}, f32[512,80]{1,0:T(8,128)S(1)}) %tuple.68), branch_computations={%region_5.6_spmd, %region_6.7_spmd} | conditional | bytes 8 | solution.py:417
  8.2 2.9 %branch_0_fun.5 = (f32[512,128]{1,0:T(8,128)S(1)}, f32[3,8,896]{2,1,0:T(8,128)S(1)}) custom-call(f32[3,800,128]{2,1,0:T(8,128)S(1)} %get-tuple-element.184.cur_ref, f32[512,80]{1,0:T(8,128)S(1)} %get-tuple-element.185.pick_ref), custom_call_target="tpu_custom_call" | custom-call | tf_op jit(solution)/shard_map/cond/branch_0_fun/pallas_call | solution.py:199
  11.1 0.9 pad_maximum_fusion.out_ref
  11.9 0.0 copy-start.1
  11.9 29.1 %shard_map.75 = (f32[512,256]{1,0:T(8,128)}, f32[3,104,128]{2,1,0:T(8,128)}, f32[3,104,128]{2,1,0:T(8,128)}, f32[3,8,896]{2,1,0:T(8,128)}, f32[3,8,896]{2,1,0:T(8,128)}) custom-call(f32[3,800,128]{2,1,0:T(8,128)S(1)} %bitcast.37, f32[3,8,896]{2,1,0:T(8,128)S(1)} %get-tuple-element.305.edges_ref, f32[512,256]{1,0:T(8,128)} %pad_maximum_fusion.out_ref), custom_call_target="tpu_custom_call" | custom-call | tf_op jit(solution)/shard_map/pallas_call | solution.py:361
  41.1 1.1 convert_reduce_fusion
  42.2 1.7 %slice.23 = f32[512,128]{1,0:T(8,128)} slice(f32[512,256]{1,0:T(8,128)} %get-tuple-element.311), slice={[0:512], [0:128]} | slice | bytes 524288 | tf_op jit(solution)/shard_map/slice | solution.py:430
  43.9 0.0 copy-done.1
  43.9 7.0 %conditional.6 = ((f32[3,800,128]{2,1,0:T(8,128)S(1)}, f32[512,128]{1,0:T(8,128)}, f32[3,8,896]{2,1,0:T(8,128)})) conditional(s32[]{:T(128)} %convert_element_type.31, (f32[3,800,128]{2,1,0:T(8,128)S(1)}, f32[3,800,128]{2,1,0:T(8,128)}, f32[2,800,128]{2,1,0:T(8,128)S(1)}, s32[800,128]{1,0:T(8,128)}, f32[3,104,128]{2,1,0:T(8,128)}, ...), branch_computations={%region_8.9_spmd, %region_9.10_spmd} | conditional | bytes 8 | solution.py:455
  43.9 6.8 %branch_0_fun.6 = (f32[3,800,128]{2,1,0:T(8,128)S(1)}, f32[512,128]{1,0:T(8,128)}, f32[3,8,896]{2,1,0:T(8,128)}) custom-call(f32[3,800,128]{2,1,0:T(8,128)S(1)} %get-tuple-element.188.cur_ref, f32[3,800,128]{2,1,0:T(8,128)} %get-tuple-element.189.prev_hbm, f32[2,800,128]{2,1,0:T(8,128)S(1)} %get-tuple-element.190.coef_hbm, ...), custom_call_target="tpu_custom_call" | custom-call | tf_op jit(solution)/shard_map/cond/branch_0_fun/pallas_call | solution.py:218
  50.9 20.6 %shard_map.76 = (f32[512,128]{1,0:T(8,128)}, f32[3,104,128]{2,1,0:T(8,128)}, f32[3,104,128]{2,1,0:T(8,128)}, f32[3,8,896]{2,1,0:T(8,128)}, f32[3,8,896]{2,1,0:T(8,128)}) custom-call(f32[3,800,128]{2,1,0:T(8,128)S(1)} %get-tuple-element.312.cur_ref, f32[3,8,896]{2,1,0:T(8,128)} %get-tuple-element.313.edges_ref, f32[512,128]{1,0:T(8,128)} %get-tuple-element.314.out_ref), custom_call_target="tpu_custom_call" | custom-call | tf_op jit(solution)/shard_map/pallas_call | solution.py:361
  71.5 7.0 %conditional.7 = ((f32[3,800,128]{2,1,0:T(8,128)}, f32[512,128]{1,0:T(8,128)}, f32[3,8,896]{2,1,0:T(8,128)})) conditional(s32[]{:T(128)} %convert_element_type.31, (f32[3,800,128]{2,1,0:T(8,128)S(1)}, f32[3,800,128]{2,1,0:T(8,128)S(1)}, f32[2,800,128]{2,1,0:T(8,128)S(1)}, s32[800,128]{1,0:T(8,128)}, f32[3,104,128]{2,1,0:T(8,128)}, ...), branch_computations={%region_10.11_spmd, %region_11.12_spmd} | conditional | bytes 8 | solution.py:455
  71.5 7.0 %branch_0_fun.7 = (f32[3,800,128]{2,1,0:T(8,128)}, f32[512,128]{1,0:T(8,128)}, f32[3,8,896]{2,1,0:T(8,128)}) custom-call(f32[3,800,128]{2,1,0:T(8,128)S(1)} %get-tuple-element.209.cur_ref, f32[3,800,128]{2,1,0:T(8,128)S(1)} %get-tuple-element.210.prev_hbm, f32[2,800,128]{2,1,0:T(8,128)S(1)} %get-tuple-element.211.coef_hbm, ...), custom_call_target="tpu_custom_call" | custom-call | tf_op jit(solution)/shard_map/cond/branch_0_fun/pallas_call | solution.py:218
  78.5 0.0 copy-start.2
  78.5 20.6 %shard_map.77 = (f32[512,128]{1,0:T(8,128)}, f32[3,104,128]{2,1,0:T(8,128)}, f32[3,104,128]{2,1,0:T(8,128)}, f32[3,8,896]{2,1,0:T(8,128)}, f32[3,8,896]{2,1,0:T(8,128)}) custom-call(f32[3,800,128]{2,1,0:T(8,128)} %get-tuple-element.320.cur_ref, f32[3,8,896]{2,1,0:T(8,128)} %get-tuple-element.321.edges_ref, f32[512,128]{1,0:T(8,128)} %get-tuple-element.322.out_ref), custom_call_target="tpu_custom_call" | custom-call | tf_op jit(solution)/shard_map/pallas_call | solution.py:361
  99.1 0.0 copy-done.2
  99.1 7.3 %conditional.8 = ((f32[3,800,128]{2,1,0:T(8,128)}, f32[512,128]{1,0:T(8,128)}, f32[3,8,896]{2,1,0:T(8,128)})) conditional(s32[]{:T(128)} %convert_element_type.31, (f32[3,800,128]{2,1,0:T(8,128)S(1)}, f32[3,800,128]{2,1,0:T(8,128)S(1)}, f32[2,800,128]{2,1,0:T(8,128)S(1)}, s32[800,128]{1,0:T(8,128)}, f32[3,104,128]{2,1,0:T(8,128)}, ...), branch_computations={%region_12.13_spmd, %region_13.14_spmd} | conditional | bytes 8 | solution.py:455
  99.3 7.0 %branch_0_fun.8 = (f32[3,800,128]{2,1,0:T(8,128)}, f32[512,128]{1,0:T(8,128)}, f32[3,8,896]{2,1,0:T(8,128)}) custom-call(f32[3,800,128]{2,1,0:T(8,128)S(1)} %get-tuple-element.230.cur_ref, f32[3,800,128]{2,1,0:T(8,128)S(1)} %get-tuple-element.231.prev_hbm, f32[2,800,128]{2,1,0:T(8,128)S(1)} %get-tuple-element.232.coef_hbm, ...), custom_call_target="tpu_custom_call" | custom-call | tf_op jit(solution)/shard_map/cond/branch_0_fun/pallas_call | solution.py:218
  106.4 0.0 copy-start.3
  106.4 20.5 %shard_map.78 = (f32[512,128]{1,0:T(8,128)}, f32[3,104,128]{2,1,0:T(8,128)}, f32[3,104,128]{2,1,0:T(8,128)}, f32[3,8,896]{2,1,0:T(8,128)}, f32[3,8,896]{2,1,0:T(8,128)}) custom-call(f32[3,800,128]{2,1,0:T(8,128)} %get-tuple-element.328.cur_ref, f32[3,8,896]{2,1,0:T(8,128)} %get-tuple-element.329.edges_ref, f32[512,128]{1,0:T(8,128)} %get-tuple-element.330.out_ref), custom_call_target="tpu_custom_call" | custom-call | tf_op jit(solution)/shard_map/pallas_call | solution.py:361
  126.8 0.0 copy-done.3
  126.8 7.0 %conditional.9 = (f32[1,3,1,1,102400]{4,3,2,1,0:T(1,128)}) conditional(s32[]{:T(128)} %convert_element_type.31, (f32[3,800,128]{2,1,0:T(8,128)S(1)}, f32[3,800,128]{2,1,0:T(8,128)S(1)}, f32[2,800,128]{2,1,0:T(8,128)S(1)}, s32[800,128]{1,0:T(8,128)}, f32[3,104,128]{2,1,0:T(8,128)}, /*index=5*/f32[3,104,128]{2,1,0:T(8,128)}, ...), branch_computations={%region_14.15_spmd, %region_15.16_spmd} | conditional | bytes 8 | solution.py:455
  126.9 7.0 %branch_0_fun.9 = (f32[3,800,128]{2,1,0:T(8,128)}, f32[512,128]{1,0:T(8,128)}, f32[3,8,896]{2,1,0:T(8,128)}) custom-call(f32[3,800,128]{2,1,0:T(8,128)S(1)} %get-tuple-element.251.cur_ref, f32[3,800,128]{2,1,0:T(8,128)S(1)} %get-tuple-element.252.prev_hbm, f32[2,800,128]{2,1,0:T(8,128)S(1)} %get-tuple-element.253.coef_hbm, ...), custom_call_target="tpu_custom_call" | custom-call | tf_op jit(solution)/shard_map/cond/branch_0_fun/pallas_call | solution.py:218
  (7 shorter events, 0.1 us)
Async XLA Ops:
  0.0 8.0 %copy-start = (f32[1,3,1,1,102400]{4,3,2,1,0:T(1,128)S(1)}, f32[1,3,1,1,102400]{4,3,2,1,0:T(1,128)}, u32[]{:S(2)}) copy-start(f32[1,3,1,1,102400]{4,3,2,1,0:T(1,128)} %param.17) | copy-start | bytes 3686404
  11.9 31.9 %copy-start.1 = (f32[1,2,1,1,102400]{4,3,2,1,0:T(1,128)S(1)}, f32[1,2,1,1,102400]{4,3,2,1,0:T(1,128)}, u32[]{:S(2)}) copy-start(f32[1,2,1,1,102400]{4,3,2,1,0:T(1,128)} %param.19) | copy-start | bytes 2457604
  78.5 20.6 %copy-start.2 = (f32[3,800,128]{2,1,0:T(8,128)S(1)}, f32[3,800,128]{2,1,0:T(8,128)}, u32[]{:S(2)}) copy-start(f32[3,800,128]{2,1,0:T(8,128)} %get-tuple-element.320.cur_ref) | copy-start | bytes 3686404
  106.4 20.5 %copy-start.3 = (f32[3,800,128]{2,1,0:T(8,128)S(1)}, f32[3,800,128]{2,1,0:T(8,128)}, u32[]{:S(2)}) copy-start(f32[3,800,128]{2,1,0:T(8,128)} %get-tuple-element.328.cur_ref) | copy-start | bytes 3686404

commit v5 on v1

--- a/solution.py
+++ b/solution.py
@@ -17,7 +17,7 @@
 ROWS = CX * NL
 BASE = 104
 PAD_ROWS = BASE + ROWS + BASE
-CHUNK = 40
+CHUNK = 80
 EDGE = 16
 HALO_ROWS = NL + 4
 EDGE_LANES = 896

time: 130 us -> 130 us (level)
  no operation moved by 1% of the time
where the time goes in v5:
time: 130 us
  Pallas kernels  117 us (90%)
  local copies, waits for them, and re-layouts  7.76 us (6%)
  other arithmetic  3.97 us (3%)
    pallas_call x4, Pallas kernels, exchange(): pl.pallas_call(functools.partial(exchange_kernel, (owners, rows_of, colum...  90.4 us
    pallas_call x4, Pallas kernels, run_step(): pl.pallas_call(kernel, out_shape=(jax.ShapeDtypeStruct((3, ROWS, CY), jnp...  24.2 us
    pallas_call x1, Pallas kernels, prepare(): pl.pallas_call(functools.partial(prepare_kernel, tiles_of), out_shape=(ja...  2.9 us

profile of v5, /device:TPU:31, one launch (start us, length us, event | category | flops | bytes accessed | tf_op | source)
XLA Modules:
  0.0 129.6 jit_solution(197255357584608261)
XLA Ops:
  0.0 0.0 copy-start
  0.0 0.8 fusion.12
  0.8 0.8 copy.12
  1.6 0.2 fusion.1
  1.9 0.9 fusion.3
  2.8 0.7 compare_select_fusion
  3.4 1.4 %scatter_custom_fusion.2 = s32[512]{0:T(512)S(1)} fusion(s32[256]{0:T(256)S(1)} %bitcast.71, s32[256]{0:T(256)S(1)} %bitcast.75, s32[]{:T(128)} %constant.9.clone.1), kind=kCustom, calls=%fused_computation.19 | custom fusion | bytes 2052 | tf_op jit(solution)/shard_map/scatter | solution.py:401
  4.9 1.4 %scatter_custom_fusion = s32[512]{0:T(512)S(1)} fusion(s32[256]{0:T(256)S(1)} %bitcast.72, s32[256]{0:T(256)S(1)} %bitcast.74, s32[]{:T(128)} %constant.10.clone.1), kind=kCustom, calls=%fused_computation.23 | custom fusion | bytes 2052 | tf_op jit(solution)/shard_map/scatter | solution.py:402
  6.3 1.6 %scatter_custom_fusion.1 = f32[512]{0:T(512)S(1)} fusion(s32[256]{0:T(256)S(1)} %bitcast.73, f32[256]{0:T(256)} %bitcast.78, f32[]{:T(128)} %constant.22.clone.1), kind=kCustom, calls=%fused_computation.21 | custom fusion | bytes 2560 | tf_op jit(solution)/shard_map/scatter | solution.py:403
  7.8 0.2 fusion
  8.0 0.0 copy-done
  8.0 0.1 broadcast_in_dim.38
  8.2 2.9 %conditional.5 = ((f32[512,128]{1,0:T(8,128)S(1)}, f32[3,8,896]{2,1,0:T(8,128)S(1)})) conditional(s32[]{:T(128)} %convert_element_type.31, (f32[3,800,128]{2,1,0:T(8,128)S(1)}, f32[512,80]{1,0:T(8,128)S(1)}) %tuple.67, (f32[3,800,128]{2,1,0:T(8,128)S(1)}, f32[512,80]{1,0:T(8,128)S(1)}) %tuple.68), branch_computations={%region_5.6_spmd, %region_6.7_spmd} | conditional | bytes 8 | solution.py:405
  8.2 2.9 %branch_0_fun.5 = (f32[512,128]{1,0:T(8,128)S(1)}, f32[3,8,896]{2,1,0:T(8,128)S(1)}) custom-call(f32[3,800,128]{2,1,0:T(8,128)S(1)} %get-tuple-element.184.cur_ref, f32[512,80]{1,0:T(8,128)S(1)} %get-tuple-element.185.pick_ref), custom_call_target="tpu_custom_call" | custom-call | tf_op jit(solution)/shard_map/cond/branch_0_fun/pallas_call | solution.py:189
  11.1 0.9 pad_maximum_fusion.out_ref
  11.9 0.0 copy-start.1
  11.9 29.1 %shard_map.75 = (f32[512,256]{1,0:T(8,128)}, f32[3,104,128]{2,1,0:T(8,128)}, f32[3,104,128]{2,1,0:T(8,128)}, f32[3,8,896]{2,1,0:T(8,128)}, f32[3,8,896]{2,1,0:T(8,128)}) custom-call(f32[3,800,128]{2,1,0:T(8,128)S(1)} %bitcast.37, f32[3,8,896]{2,1,0:T(8,128)S(1)} %get-tuple-element.305.edges_ref, f32[512,256]{1,0:T(8,128)} %pad_maximum_fusion.out_ref), custom_call_target="tpu_custom_call" | custom-call | tf_op jit(solution)/shard_map/pallas_call | solution.py:349
  41.1 1.1 convert_reduce_fusion
  42.2 1.7 %slice.23 = f32[512,128]{1,0:T(8,128)} slice(f32[512,256]{1,0:T(8,128)} %get-tuple-element.311), slice={[0:512], [0:128]} | slice | bytes 524288 | tf_op jit(solution)/shard_map/slice | solution.py:418
  43.9 0.0 copy-done.1
  43.9 6.3 %conditional.6 = ((f32[3,800,128]{2,1,0:T(8,128)S(1)}, f32[512,128]{1,0:T(8,128)}, f32[3,8,896]{2,1,0:T(8,128)})) conditional(s32[]{:T(128)} %convert_element_type.31, (f32[3,800,128]{2,1,0:T(8,128)S(1)}, f32[3,800,128]{2,1,0:T(8,128)}, f32[2,800,128]{2,1,0:T(8,128)S(1)}, s32[800,128]{1,0:T(8,128)}, f32[3,104,128]{2,1,0:T(8,128)}, ...), branch_computations={%region_8.9_spmd, %region_9.10_spmd} | conditional | bytes 8 | solution.py:439
  43.9 6.3 %branch_0_fun.6 = (f32[3,800,128]{2,1,0:T(8,128)S(1)}, f32[512,128]{1,0:T(8,128)}, f32[3,8,896]{2,1,0:T(8,128)}) custom-call(f32[3,800,128]{2,1,0:T(8,128)S(1)} %get-tuple-element.188.cur_ref, f32[3,800,128]{2,1,0:T(8,128)} %get-tuple-element.189.prev_ref, f32[2,800,128]{2,1,0:T(8,128)S(1)} %get-tuple-element.190.coef_ref, ...), custom_call_target="tpu_custom_call" | custom-call | tf_op jit(solution)/shard_map/cond/branch_0_fun/pallas_call | solution.py:206
  50.2 20.5 %shard_map.76 = (f32[512,128]{1,0:T(8,128)}, f32[3,104,128]{2,1,0:T(8,128)}, f32[3,104,128]{2,1,0:T(8,128)}, f32[3,8,896]{2,1,0:T(8,128)}, f32[3,8,896]{2,1,0:T(8,128)}) custom-call(f32[3,800,128]{2,1,0:T(8,128)S(1)} %get-tuple-element.312.cur_ref, f32[3,8,896]{2,1,0:T(8,128)} %get-tuple-element.313.edges_ref, f32[512,128]{1,0:T(8,128)} %get-tuple-element.314.out_ref), custom_call_target="tpu_custom_call" | custom-call | tf_op jit(solution)/shard_map/pallas_call | solution.py:349
  70.6 6.0 %conditional.7 = ((f32[3,800,128]{2,1,0:T(8,128)}, f32[512,128]{1,0:T(8,128)}, f32[3,8,896]{2,1,0:T(8,128)})) conditional(s32[]{:T(128)} %convert_element_type.31, (f32[3,800,128]{2,1,0:T(8,128)S(1)}, f32[3,800,128]{2,1,0:T(8,128)S(1)}, f32[2,800,128]{2,1,0:T(8,128)S(1)}, s32[800,128]{1,0:T(8,128)}, f32[3,104,128]{2,1,0:T(8,128)}, ...), branch_computations={%region_10.11_spmd, %region_11.12_spmd} | conditional | bytes 8 | solution.py:439
  70.7 6.0 %branch_0_fun.7 = (f32[3,800,128]{2,1,0:T(8,128)}, f32[512,128]{1,0:T(8,128)}, f32[3,8,896]{2,1,0:T(8,128)}) custom-call(f32[3,800,128]{2,1,0:T(8,128)S(1)} %get-tuple-element.209.cur_ref, f32[3,800,128]{2,1,0:T(8,128)S(1)} %get-tuple-element.210.prev_ref, f32[2,800,128]{2,1,0:T(8,128)S(1)} %get-tuple-element.211.coef_ref, ...), custom_call_target="tpu_custom_call" | custom-call | tf_op jit(solution)/shard_map/cond/branch_0_fun/pallas_call | solution.py:206
  76.6 0.0 copy-start.2
  76.6 20.4 %shard_map.77 = (f32[512,128]{1,0:T(8,128)}, f32[3,104,128]{2,1,0:T(8,128)}, f32[3,104,128]{2,1,0:T(8,128)}, f32[3,8,896]{2,1,0:T(8,128)}, f32[3,8,896]{2,1,0:T(8,128)}) custom-call(f32[3,800,128]{2,1,0:T(8,128)} %get-tuple-element.320.cur_ref, f32[3,8,896]{2,1,0:T(8,128)} %get-tuple-element.321.edges_ref, f32[512,128]{1,0:T(8,128)} %get-tuple-element.322.out_ref), custom_call_target="tpu_custom_call" | custom-call | tf_op jit(solution)/shard_map/pallas_call | solution.py:349
  97.1 0.0 copy-done.2
  97.1 6.2 %conditional.8 = ((f32[3,800,128]{2,1,0:T(8,128)}, f32[512,128]{1,0:T(8,128)}, f32[3,8,896]{2,1,0:T(8,128)})) conditional(s32[]{:T(128)} %convert_element_type.31, (f32[3,800,128]{2,1,0:T(8,128)S(1)}, f32[3,800,128]{2,1,0:T(8,128)S(1)}, f32[2,800,128]{2,1,0:T(8,128)S(1)}, s32[800,128]{1,0:T(8,128)}, f32[3,104,128]{2,1,0:T(8,128)}, ...), branch_computations={%region_12.13_spmd, %region_13.14_spmd} | conditional | bytes 8 | solution.py:439
  97.3 6.0 %branch_0_fun.8 = (f32[3,800,128]{2,1,0:T(8,128)}, f32[512,128]{1,0:T(8,128)}, f32[3,8,896]{2,1,0:T(8,128)}) custom-call(f32[3,800,128]{2,1,0:T(8,128)S(1)} %get-tuple-element.230.cur_ref, f32[3,800,128]{2,1,0:T(8,128)S(1)} %get-tuple-element.231.prev_ref, f32[2,800,128]{2,1,0:T(8,128)S(1)} %get-tuple-element.232.coef_ref, ...), custom_call_target="tpu_custom_call" | custom-call | tf_op jit(solution)/shard_map/cond/branch_0_fun/pallas_call | solution.py:206
  103.3 0.0 copy-start.3
  103.3 20.3 %shard_map.78 = (f32[512,128]{1,0:T(8,128)}, f32[3,104,128]{2,1,0:T(8,128)}, f32[3,104,128]{2,1,0:T(8,128)}, f32[3,8,896]{2,1,0:T(8,128)}, f32[3,8,896]{2,1,0:T(8,128)}) custom-call(f32[3,800,128]{2,1,0:T(8,128)} %get-tuple-element.328.cur_ref, f32[3,8,896]{2,1,0:T(8,128)} %get-tuple-element.329.edges_ref, f32[512,128]{1,0:T(8,128)} %get-tuple-element.330.out_ref), custom_call_target="tpu_custom_call" | custom-call | tf_op jit(solution)/shard_map/pallas_call | solution.py:349
  123.6 0.0 copy-done.3
  123.6 6.0 %conditional.9 = (f32[1,3,1,1,102400]{4,3,2,1,0:T(1,128)}) conditional(s32[]{:T(128)} %convert_element_type.31, (f32[3,800,128]{2,1,0:T(8,128)S(1)}, f32[3,800,128]{2,1,0:T(8,128)S(1)}, f32[2,800,128]{2,1,0:T(8,128)S(1)}, s32[800,128]{1,0:T(8,128)}, f32[3,104,128]{2,1,0:T(8,128)}, /*index=5*/f32[3,104,128]{2,1,0:T(8,128)}, ...), branch_computations={%region_14.15_spmd, %region_15.16_spmd} | conditional | bytes 8 | solution.py:439
  123.7 6.0 %branch_0_fun.9 = (f32[3,800,128]{2,1,0:T(8,128)}, f32[512,128]{1,0:T(8,128)}, f32[3,8,896]{2,1,0:T(8,128)}) custom-call(f32[3,800,128]{2,1,0:T(8,128)S(1)} %get-tuple-element.251.cur_ref, f32[3,800,128]{2,1,0:T(8,128)S(1)} %get-tuple-element.252.prev_ref, f32[2,800,128]{2,1,0:T(8,128)S(1)} %get-tuple-element.253.coef_ref, ...), custom_call_target="tpu_custom_call" | custom-call | tf_op jit(solution)/shard_map/cond/branch_0_fun/pallas_call | solution.py:206
  (7 shorter events, 0.1 us)
Async XLA Ops:
  0.0 8.0 %copy-start = (f32[1,3,1,1,102400]{4,3,2,1,0:T(1,128)S(1)}, f32[1,3,1,1,102400]{4,3,2,1,0:T(1,128)}, u32[]{:S(2)}) copy-start(f32[1,3,1,1,102400]{4,3,2,1,0:T(1,128)} %param.17) | copy-start | bytes 3686404
  11.9 31.9 %copy-start.1 = (f32[1,2,1,1,102400]{4,3,2,1,0:T(1,128)S(1)}, f32[1,2,1,1,102400]{4,3,2,1,0:T(1,128)}, u32[]{:S(2)}) copy-start(f32[1,2,1,1,102400]{4,3,2,1,0:T(1,128)} %param.19) | copy-start | bytes 2457604
  76.6 20.4 %copy-start.2 = (f32[3,800,128]{2,1,0:T(8,128)S(1)}, f32[3,800,128]{2,1,0:T(8,128)}, u32[]{:S(2)}) copy-start(f32[3,800,128]{2,1,0:T(8,128)} %get-tuple-element.320.cur_ref) | copy-start | bytes 3686404
  103.3 20.3 %copy-start.3 = (f32[3,800,128]{2,1,0:T(8,128)S(1)}, f32[3,800,128]{2,1,0:T(8,128)}, u32[]{:S(2)}) copy-start(f32[3,800,128]{2,1,0:T(8,128)} %get-tuple-element.328.cur_ref) | copy-start | bytes 3686404

commit v6 on v1

--- a/solution.py
+++ b/solution.py
@@ -236,7 +236,7 @@
                             device_id_type=pl.DeviceIdType.MESH)
         return carry
 
-    lax.fori_loop(0, owners, greet, 0, unroll=8)
+    lax.fori_loop(0, owners, greet, 0, unroll=True)
 
     @pl.when(has_low)
     def _():
@@ -304,7 +304,7 @@
         ).start()
         return carry
 
-    lax.fori_loop(0, owners, send, 0, unroll=8)
+    lax.fori_loop(0, owners, send, 0, unroll=True)
     whole = pltpu.make_async_remote_copy(
         src_ref=out_ref,
         dst_ref=land,

time: 130 us -> 129 us (level)
  no operation moved by 1% of the time
where the time goes in v6:
time: 129 us
  Pallas kernels  117 us (91%)
  local copies, waits for them, and re-layouts  7.76 us (6%)
  other arithmetic  3.97 us (3%)
    pallas_call x4, Pallas kernels, exchange(): pl.pallas_call(functools.partial(exchange_kernel, (owners, rows_of, colum...  89.6 us
    pallas_call x4, Pallas kernels, run_step(): pl.pallas_call(kernel, out_shape=(jax.ShapeDtypeStruct((3, ROWS, CY), jnp...  24.2 us
    pallas_call x1, Pallas kernels, prepare(): pl.pallas_call(functools.partial(prepare_kernel, tiles_of), out_shape=(ja...  2.9 us

profile of v6, /device:TPU:31, one launch (start us, length us, event | category | flops | bytes accessed | tf_op | source)
XLA Modules:
  0.0 128.8 jit_solution(14881735020464823369)
XLA Ops:
  0.0 0.0 copy-start
  0.0 0.8 fusion.12
  0.8 0.8 copy.12
  1.6 0.2 fusion.1
  1.9 0.9 fusion.3
  2.8 0.7 compare_select_fusion
  3.4 1.4 %scatter_custom_fusion.2 = s32[512]{0:T(512)S(1)} fusion(s32[256]{0:T(256)S(1)} %bitcast.71, s32[256]{0:T(256)S(1)} %bitcast.75, s32[]{:T(128)} %constant.9.clone.1), kind=kCustom, calls=%fused_computation.19 | custom fusion | bytes 2052 | tf_op jit(solution)/shard_map/scatter | solution.py:401
  4.9 1.4 %scatter_custom_fusion = s32[512]{0:T(512)S(1)} fusion(s32[256]{0:T(256)S(1)} %bitcast.72, s32[256]{0:T(256)S(1)} %bitcast.74, s32[]{:T(128)} %constant.10.clone.1), kind=kCustom, calls=%fused_computation.23 | custom fusion | bytes 2052 | tf_op jit(solution)/shard_map/scatter | solution.py:402
  6.3 1.6 %scatter_custom_fusion.1 = f32[512]{0:T(512)S(1)} fusion(s32[256]{0:T(256)S(1)} %bitcast.73, f32[256]{0:T(256)} %bitcast.78, f32[]{:T(128)} %constant.22.clone.1), kind=kCustom, calls=%fused_computation.21 | custom fusion | bytes 2560 | tf_op jit(solution)/shard_map/scatter | solution.py:403
  7.8 0.2 fusion
  8.0 0.0 copy-done
  8.0 0.1 broadcast_in_dim.38
  8.2 2.9 %conditional.5 = ((f32[512,128]{1,0:T(8,128)S(1)}, f32[3,8,896]{2,1,0:T(8,128)S(1)})) conditional(s32[]{:T(128)} %convert_element_type.31, (f32[3,800,128]{2,1,0:T(8,128)S(1)}, f32[512,80]{1,0:T(8,128)S(1)}) %tuple.67, (f32[3,800,128]{2,1,0:T(8,128)S(1)}, f32[512,80]{1,0:T(8,128)S(1)}) %tuple.68), branch_computations={%region_5.6_spmd, %region_6.7_spmd} | conditional | bytes 8 | solution.py:405
  8.2 2.9 %branch_0_fun.5 = (f32[512,128]{1,0:T(8,128)S(1)}, f32[3,8,896]{2,1,0:T(8,128)S(1)}) custom-call(f32[3,800,128]{2,1,0:T(8,128)S(1)} %get-tuple-element.184.cur_ref, f32[512,80]{1,0:T(8,128)S(1)} %get-tuple-element.185.pick_ref), custom_call_target="tpu_custom_call" | custom-call | tf_op jit(solution)/shard_map/cond/branch_0_fun/pallas_call | solution.py:189
  11.1 0.9 pad_maximum_fusion.out_ref
  11.9 0.0 copy-start.1
  11.9 29.0 %shard_map.75 = (f32[512,256]{1,0:T(8,128)}, f32[3,104,128]{2,1,0:T(8,128)}, f32[3,104,128]{2,1,0:T(8,128)}, f32[3,8,896]{2,1,0:T(8,128)}, f32[3,8,896]{2,1,0:T(8,128)}) custom-call(f32[3,800,128]{2,1,0:T(8,128)S(1)} %bitcast.37, f32[3,8,896]{2,1,0:T(8,128)S(1)} %get-tuple-element.305.edges_ref, f32[512,256]{1,0:T(8,128)} %pad_maximum_fusion.out_ref), custom_call_target="tpu_custom_call" | custom-call | tf_op jit(solution)/shard_map/pallas_call | solution.py:349
  40.9 1.1 convert_reduce_fusion
  42.0 1.7 %slice.23 = f32[512,128]{1,0:T(8,128)} slice(f32[512,256]{1,0:T(8,128)} %get-tuple-element.311), slice={[0:512], [0:128]} | slice | bytes 524288 | tf_op jit(solution)/shard_map/slice | solution.py:418
  43.7 0.0 copy-done.1
  43.7 6.3 %conditional.6 = ((f32[3,800,128]{2,1,0:T(8,128)S(1)}, f32[512,128]{1,0:T(8,128)}, f32[3,8,896]{2,1,0:T(8,128)})) conditional(s32[]{:T(128)} %convert_element_type.31, (f32[3,800,128]{2,1,0:T(8,128)S(1)}, f32[3,800,128]{2,1,0:T(8,128)}, f32[2,800,128]{2,1,0:T(8,128)S(1)}, s32[800,128]{1,0:T(8,128)}, f32[3,104,128]{2,1,0:T(8,128)}, ...), branch_computations={%region_8.9_spmd, %region_9.10_spmd} | conditional | bytes 8 | solution.py:439
  43.7 6.3 %branch_0_fun.6 = (f32[3,800,128]{2,1,0:T(8,128)S(1)}, f32[512,128]{1,0:T(8,128)}, f32[3,8,896]{2,1,0:T(8,128)}) custom-call(f32[3,800,128]{2,1,0:T(8,128)S(1)} %get-tuple-element.188.cur_ref, f32[3,800,128]{2,1,0:T(8,128)} %get-tuple-element.189.prev_ref, f32[2,800,128]{2,1,0:T(8,128)S(1)} %get-tuple-element.190.coef_ref, ...), custom_call_target="tpu_custom_call" | custom-call | tf_op jit(solution)/shard_map/cond/branch_0_fun/pallas_call | solution.py:206
  50.0 20.2 %shard_map.76 = (f32[512,128]{1,0:T(8,128)}, f32[3,104,128]{2,1,0:T(8,128)}, f32[3,104,128]{2,1,0:T(8,128)}, f32[3,8,896]{2,1,0:T(8,128)}, f32[3,8,896]{2,1,0:T(8,128)}) custom-call(f32[3,800,128]{2,1,0:T(8,128)S(1)} %get-tuple-element.312.cur_ref, f32[3,8,896]{2,1,0:T(8,128)} %get-tuple-element.313.edges_ref, f32[512,128]{1,0:T(8,128)} %get-tuple-element.314.out_ref), custom_call_target="tpu_custom_call" | custom-call | tf_op jit(solution)/shard_map/pallas_call | solution.py:349
  70.2 6.0 %conditional.7 = ((f32[3,800,128]{2,1,0:T(8,128)}, f32[512,128]{1,0:T(8,128)}, f32[3,8,896]{2,1,0:T(8,128)})) conditional(s32[]{:T(128)} %convert_element_type.31, (f32[3,800,128]{2,1,0:T(8,128)S(1)}, f32[3,800,128]{2,1,0:T(8,128)S(1)}, f32[2,800,128]{2,1,0:T(8,128)S(1)}, s32[800,128]{1,0:T(8,128)}, f32[3,104,128]{2,1,0:T(8,128)}, ...), branch_computations={%region_10.11_spmd, %region_11.12_spmd} | conditional | bytes 8 | solution.py:439
  70.3 6.0 %branch_0_fun.7 = (f32[3,800,128]{2,1,0:T(8,128)}, f32[512,128]{1,0:T(8,128)}, f32[3,8,896]{2,1,0:T(8,128)}) custom-call(f32[3,800,128]{2,1,0:T(8,128)S(1)} %get-tuple-element.209.cur_ref, f32[3,800,128]{2,1,0:T(8,128)S(1)} %get-tuple-element.210.prev_ref, f32[2,800,128]{2,1,0:T(8,128)S(1)} %get-tuple-element.211.coef_ref, ...), custom_call_target="tpu_custom_call" | custom-call | tf_op jit(solution)/shard_map/cond/branch_0_fun/pallas_call | solution.py:206
  76.2 0.0 copy-start.2
  76.2 20.2 %shard_map.77 = (f32[512,128]{1,0:T(8,128)}, f32[3,104,128]{2,1,0:T(8,128)}, f32[3,104,128]{2,1,0:T(8,128)}, f32[3,8,896]{2,1,0:T(8,128)}, f32[3,8,896]{2,1,0:T(8,128)}) custom-call(f32[3,800,128]{2,1,0:T(8,128)} %get-tuple-element.320.cur_ref, f32[3,8,896]{2,1,0:T(8,128)} %get-tuple-element.321.edges_ref, f32[512,128]{1,0:T(8,128)} %get-tuple-element.322.out_ref), custom_call_target="tpu_custom_call" | custom-call | tf_op jit(solution)/shard_map/pallas_call | solution.py:349
  96.5 0.0 copy-done.2
  96.5 6.2 %conditional.8 = ((f32[3,800,128]{2,1,0:T(8,128)}, f32[512,128]{1,0:T(8,128)}, f32[3,8,896]{2,1,0:T(8,128)})) conditional(s32[]{:T(128)} %convert_element_type.31, (f32[3,800,128]{2,1,0:T(8,128)S(1)}, f32[3,800,128]{2,1,0:T(8,128)S(1)}, f32[2,800,128]{2,1,0:T(8,128)S(1)}, s32[800,128]{1,0:T(8,128)}, f32[3,104,128]{2,1,0:T(8,128)}, ...), branch_computations={%region_12.13_spmd, %region_13.14_spmd} | conditional | bytes 8 | solution.py:439
  96.7 6.0 %branch_0_fun.8 = (f32[3,800,128]{2,1,0:T(8,128)}, f32[512,128]{1,0:T(8,128)}, f32[3,8,896]{2,1,0:T(8,128)}) custom-call(f32[3,800,128]{2,1,0:T(8,128)S(1)} %get-tuple-element.230.cur_ref, f32[3,800,128]{2,1,0:T(8,128)S(1)} %get-tuple-element.231.prev_ref, f32[2,800,128]{2,1,0:T(8,128)S(1)} %get-tuple-element.232.coef_ref, ...), custom_call_target="tpu_custom_call" | custom-call | tf_op jit(solution)/shard_map/cond/branch_0_fun/pallas_call | solution.py:206
  102.7 0.0 copy-start.3
  102.7 20.1 %shard_map.78 = (f32[512,128]{1,0:T(8,128)}, f32[3,104,128]{2,1,0:T(8,128)}, f32[3,104,128]{2,1,0:T(8,128)}, f32[3,8,896]{2,1,0:T(8,128)}, f32[3,8,896]{2,1,0:T(8,128)}) custom-call(f32[3,800,128]{2,1,0:T(8,128)} %get-tuple-element.328.cur_ref, f32[3,8,896]{2,1,0:T(8,128)} %get-tuple-element.329.edges_ref, f32[512,128]{1,0:T(8,128)} %get-tuple-element.330.out_ref), custom_call_target="tpu_custom_call" | custom-call | tf_op jit(solution)/shard_map/pallas_call | solution.py:349
  122.8 0.0 copy-done.3
  122.8 6.0 %conditional.9 = (f32[1,3,1,1,102400]{4,3,2,1,0:T(1,128)}) conditional(s32[]{:T(128)} %convert_element_type.31, (f32[3,800,128]{2,1,0:T(8,128)S(1)}, f32[3,800,128]{2,1,0:T(8,128)S(1)}, f32[2,800,128]{2,1,0:T(8,128)S(1)}, s32[800,128]{1,0:T(8,128)}, f32[3,104,128]{2,1,0:T(8,128)}, /*index=5*/f32[3,104,128]{2,1,0:T(8,128)}, ...), branch_computations={%region_14.15_spmd, %region_15.16_spmd} | conditional | bytes 8 | solution.py:439
  122.8 6.0 %branch_0_fun.9 = (f32[3,800,128]{2,1,0:T(8,128)}, f32[512,128]{1,0:T(8,128)}, f32[3,8,896]{2,1,0:T(8,128)}) custom-call(f32[3,800,128]{2,1,0:T(8,128)S(1)} %get-tuple-element.251.cur_ref, f32[3,800,128]{2,1,0:T(8,128)S(1)} %get-tuple-element.252.prev_ref, f32[2,800,128]{2,1,0:T(8,128)S(1)} %get-tuple-element.253.coef_ref, ...), custom_call_target="tpu_custom_call" | custom-call | tf_op jit(solution)/shard_map/cond/branch_0_fun/pallas_call | solution.py:206
  (7 shorter events, 0.1 us)
Async XLA Ops:
  0.0 8.0 %copy-start = (f32[1,3,1,1,102400]{4,3,2,1,0:T(1,128)S(1)}, f32[1,3,1,1,102400]{4,3,2,1,0:T(1,128)}, u32[]{:S(2)}) copy-start(f32[1,3,1,1,102400]{4,3,2,1,0:T(1,128)} %param.17) | copy-start | bytes 3686404
  11.9 31.7 %copy-start.1 = (f32[1,2,1,1,102400]{4,3,2,1,0:T(1,128)S(1)}, f32[1,2,1,1,102400]{4,3,2,1,0:T(1,128)}, u32[]{:S(2)}) copy-start(f32[1,2,1,1,102400]{4,3,2,1,0:T(1,128)} %param.19) | copy-start | bytes 2457604
  76.2 20.2 %copy-start.2 = (f32[3,800,128]{2,1,0:T(8,128)S(1)}, f32[3,800,128]{2,1,0:T(8,128)}, u32[]{:S(2)}) copy-start(f32[3,800,128]{2,1,0:T(8,128)} %get-tuple-element.320.cur_ref) | copy-start | bytes 3686404
  102.7 20.2 %copy-start.3 = (f32[3,800,128]{2,1,0:T(8,128)S(1)}, f32[3,800,128]{2,1,0:T(8,128)}, u32[]{:S(2)}) copy-start(f32[3,800,128]{2,1,0:T(8,128)} %get-tuple-element.328.cur_ref) | copy-start | bytes 3686404

commit v7 on v6

--- a/solution.py
+++ b/solution.py
@@ -73,7 +73,7 @@
     lanes = lax.broadcasted_iota(jnp.int32, (8, CY), 1)
     select = (((rows == 0) & (lanes == CY - 1)) | ((rows == 1) & (lanes == 0))).astype(jnp.float32)
     for f in range(3):
-        picked = lax.dot_general(select, out_ref[f], (((1,), (1,)), ((), ())), precision=lax.Precision.HIGHEST,
+        picked = lax.dot_general(select, out_ref[f], (((1,), (1,)), ((), ())), precision=lax.Precision.HIGH,
                                  preferred_element_type=jnp.float32)
         edges_ref[f] = jnp.zeros(edges_ref.shape[1:], jnp.float32)
         edges_ref[f, :, pl.ds(0, ROWS)] = picked

time: 129 us -> 127 us (0.984)
  Pallas kernels: 117 us -> 114 us
    pallas_call x4, Pallas kernels: 24.2 us -> 22.4 us  [run_step(): pl.pallas_call(kernel, out_shape=(jax.ShapeDtypeStruct((3, ROWS, CY), jnp...]
where the time goes in v7:
time: 127 us
  Pallas kernels  114 us (90%)
  local copies, waits for them, and re-layouts  7.76 us (6%)
  other arithmetic  3.96 us (3%)
    pallas_call x4, Pallas kernels, exchange(): pl.pallas_call(functools.partial(exchange_kernel, (owners, rows_of, colum...  89.6 us
    pallas_call x4, Pallas kernels, run_step(): pl.pallas_call(kernel, out_shape=(jax.ShapeDtypeStruct((3, ROWS, CY), jnp...  22.4 us

profile of v7, /device:TPU:31, one launch (start us, length us, event | category | flops | bytes accessed | tf_op | source)
XLA Modules:
  0.0 126.5 jit_solution(5741795619893057987)
XLA Ops:
  0.0 0.0 copy-start
  0.0 0.8 fusion.12
  0.8 0.8 copy.12
  1.6 0.2 fusion.1
  1.9 0.9 fusion.3
  2.8 0.7 compare_select_fusion
  3.4 1.4 %scatter_custom_fusion.2 = s32[512]{0:T(512)S(1)} fusion(s32[256]{0:T(256)S(1)} %bitcast.71, s32[256]{0:T(256)S(1)} %bitcast.75, s32[]{:T(128)} %constant.9.clone.1), kind=kCustom, calls=%fused_computation.19 | custom fusion | bytes 2052 | tf_op jit(solution)/shard_map/scatter | solution.py:401
  4.9 1.4 %scatter_custom_fusion = s32[512]{0:T(512)S(1)} fusion(s32[256]{0:T(256)S(1)} %bitcast.72, s32[256]{0:T(256)S(1)} %bitcast.74, s32[]{:T(128)} %constant.10.clone.1), kind=kCustom, calls=%fused_computation.23 | custom fusion | bytes 2052 | tf_op jit(solution)/shard_map/scatter | solution.py:402
  6.3 1.6 %scatter_custom_fusion.1 = f32[512]{0:T(512)S(1)} fusion(s32[256]{0:T(256)S(1)} %bitcast.73, f32[256]{0:T(256)} %bitcast.78, f32[]{:T(128)} %constant.22.clone.1), kind=kCustom, calls=%fused_computation.21 | custom fusion | bytes 2560 | tf_op jit(solution)/shard_map/scatter | solution.py:403
  7.8 0.2 fusion
  8.0 0.0 copy-done
  8.0 0.1 broadcast_in_dim.38
  8.2 2.4 %conditional.5 = ((f32[512,128]{1,0:T(8,128)S(1)}, f32[3,8,896]{2,1,0:T(8,128)S(1)})) conditional(s32[]{:T(128)} %convert_element_type.31, (f32[3,800,128]{2,1,0:T(8,128)S(1)}, f32[512,80]{1,0:T(8,128)S(1)}) %tuple.67, (f32[3,800,128]{2,1,0:T(8,128)S(1)}, f32[512,80]{1,0:T(8,128)S(1)}) %tuple.68), branch_computations={%region_5.6_spmd, %region_6.7_spmd} | conditional | bytes 8 | solution.py:405
  8.2 2.4 %branch_0_fun.5 = (f32[512,128]{1,0:T(8,128)S(1)}, f32[3,8,896]{2,1,0:T(8,128)S(1)}) custom-call(f32[3,800,128]{2,1,0:T(8,128)S(1)} %get-tuple-element.184.cur_ref, f32[512,80]{1,0:T(8,128)S(1)} %get-tuple-element.185.pick_ref), custom_call_target="tpu_custom_call" | custom-call | tf_op jit(solution)/shard_map/cond/branch_0_fun/pallas_call | solution.py:189
  10.6 0.9 pad_maximum_fusion.out_ref
  11.5 0.0 copy-start.1
  11.5 29.0 %shard_map.75 = (f32[512,256]{1,0:T(8,128)}, f32[3,104,128]{2,1,0:T(8,128)}, f32[3,104,128]{2,1,0:T(8,128)}, f32[3,8,896]{2,1,0:T(8,128)}, f32[3,8,896]{2,1,0:T(8,128)}) custom-call(f32[3,800,128]{2,1,0:T(8,128)S(1)} %bitcast.37, f32[3,8,896]{2,1,0:T(8,128)S(1)} %get-tuple-element.305.edges_ref, f32[512,256]{1,0:T(8,128)} %pad_maximum_fusion.out_ref), custom_call_target="tpu_custom_call" | custom-call | tf_op jit(solution)/shard_map/pallas_call | solution.py:349
  40.4 1.1 convert_reduce_fusion
  41.5 1.7 %slice.23 = f32[512,128]{1,0:T(8,128)} slice(f32[512,256]{1,0:T(8,128)} %get-tuple-element.311), slice={[0:512], [0:128]} | slice | bytes 524288 | tf_op jit(solution)/shard_map/slice | solution.py:418
  43.2 0.0 copy-done.1
  43.2 5.8 %conditional.6 = ((f32[3,800,128]{2,1,0:T(8,128)S(1)}, f32[512,128]{1,0:T(8,128)}, f32[3,8,896]{2,1,0:T(8,128)})) conditional(s32[]{:T(128)} %convert_element_type.31, (f32[3,800,128]{2,1,0:T(8,128)S(1)}, f32[3,800,128]{2,1,0:T(8,128)}, f32[2,800,128]{2,1,0:T(8,128)S(1)}, s32[800,128]{1,0:T(8,128)}, f32[3,104,128]{2,1,0:T(8,128)}, ...), branch_computations={%region_8.9_spmd, %region_9.10_spmd} | conditional | bytes 8 | solution.py:439
  43.2 5.8 %branch_0_fun.6 = (f32[3,800,128]{2,1,0:T(8,128)S(1)}, f32[512,128]{1,0:T(8,128)}, f32[3,8,896]{2,1,0:T(8,128)}) custom-call(f32[3,800,128]{2,1,0:T(8,128)S(1)} %get-tuple-element.188.cur_ref, f32[3,800,128]{2,1,0:T(8,128)} %get-tuple-element.189.prev_ref, f32[2,800,128]{2,1,0:T(8,128)S(1)} %get-tuple-element.190.coef_ref, ...), custom_call_target="tpu_custom_call" | custom-call | tf_op jit(solution)/shard_map/cond/branch_0_fun/pallas_call | solution.py:206
  49.0 20.2 %shard_map.76 = (f32[512,128]{1,0:T(8,128)}, f32[3,104,128]{2,1,0:T(8,128)}, f32[3,104,128]{2,1,0:T(8,128)}, f32[3,8,896]{2,1,0:T(8,128)}, f32[3,8,896]{2,1,0:T(8,128)}) custom-call(f32[3,800,128]{2,1,0:T(8,128)S(1)} %get-tuple-element.312.cur_ref, f32[3,8,896]{2,1,0:T(8,128)} %get-tuple-element.313.edges_ref, f32[512,128]{1,0:T(8,128)} %get-tuple-element.314.out_ref), custom_call_target="tpu_custom_call" | custom-call | tf_op jit(solution)/shard_map/pallas_call | solution.py:349
  69.3 5.5 %conditional.7 = ((f32[3,800,128]{2,1,0:T(8,128)}, f32[512,128]{1,0:T(8,128)}, f32[3,8,896]{2,1,0:T(8,128)})) conditional(s32[]{:T(128)} %convert_element_type.31, (f32[3,800,128]{2,1,0:T(8,128)S(1)}, f32[3,800,128]{2,1,0:T(8,128)S(1)}, f32[2,800,128]{2,1,0:T(8,128)S(1)}, s32[800,128]{1,0:T(8,128)}, f32[3,104,128]{2,1,0:T(8,128)}, ...), branch_computations={%region_10.11_spmd, %region_11.12_spmd} | conditional | bytes 8 | solution.py:439
  69.3 5.5 %branch_0_fun.7 = (f32[3,800,128]{2,1,0:T(8,128)}, f32[512,128]{1,0:T(8,128)}, f32[3,8,896]{2,1,0:T(8,128)}) custom-call(f32[3,800,128]{2,1,0:T(8,128)S(1)} %get-tuple-element.209.cur_ref, f32[3,800,128]{2,1,0:T(8,128)S(1)} %get-tuple-element.210.prev_ref, f32[2,800,128]{2,1,0:T(8,128)S(1)} %get-tuple-element.211.coef_ref, ...), custom_call_target="tpu_custom_call" | custom-call | tf_op jit(solution)/shard_map/cond/branch_0_fun/pallas_call | solution.py:206
  74.8 0.0 copy-start.2
  74.8 20.2 %shard_map.77 = (f32[512,128]{1,0:T(8,128)}, f32[3,104,128]{2,1,0:T(8,128)}, f32[3,104,128]{2,1,0:T(8,128)}, f32[3,8,896]{2,1,0:T(8,128)}, f32[3,8,896]{2,1,0:T(8,128)}) custom-call(f32[3,800,128]{2,1,0:T(8,128)} %get-tuple-element.320.cur_ref, f32[3,8,896]{2,1,0:T(8,128)} %get-tuple-element.321.edges_ref, f32[512,128]{1,0:T(8,128)} %get-tuple-element.322.out_ref), custom_call_target="tpu_custom_call" | custom-call | tf_op jit(solution)/shard_map/pallas_call | solution.py:349
  95.1 0.0 copy-done.2
  95.1 5.7 %conditional.8 = ((f32[3,800,128]{2,1,0:T(8,128)}, f32[512,128]{1,0:T(8,128)}, f32[3,8,896]{2,1,0:T(8,128)})) conditional(s32[]{:T(128)} %convert_element_type.31, (f32[3,800,128]{2,1,0:T(8,128)S(1)}, f32[3,800,128]{2,1,0:T(8,128)S(1)}, f32[2,800,128]{2,1,0:T(8,128)S(1)}, s32[800,128]{1,0:T(8,128)}, f32[3,104,128]{2,1,0:T(8,128)}, ...), branch_computations={%region_12.13_spmd, %region_13.14_spmd} | conditional | bytes 8 | solution.py:439
  95.3 5.5 %branch_0_fun.8 = (f32[3,800,128]{2,1,0:T(8,128)}, f32[512,128]{1,0:T(8,128)}, f32[3,8,896]{2,1,0:T(8,128)}) custom-call(f32[3,800,128]{2,1,0:T(8,128)S(1)} %get-tuple-element.230.cur_ref, f32[3,800,128]{2,1,0:T(8,128)S(1)} %get-tuple-element.231.prev_ref, f32[2,800,128]{2,1,0:T(8,128)S(1)} %get-tuple-element.232.coef_ref, ...), custom_call_target="tpu_custom_call" | custom-call | tf_op jit(solution)/shard_map/cond/branch_0_fun/pallas_call | solution.py:206
  100.8 0.0 copy-start.3
  100.8 20.2 %shard_map.78 = (f32[512,128]{1,0:T(8,128)}, f32[3,104,128]{2,1,0:T(8,128)}, f32[3,104,128]{2,1,0:T(8,128)}, f32[3,8,896]{2,1,0:T(8,128)}, f32[3,8,896]{2,1,0:T(8,128)}) custom-call(f32[3,800,128]{2,1,0:T(8,128)} %get-tuple-element.328.cur_ref, f32[3,8,896]{2,1,0:T(8,128)} %get-tuple-element.329.edges_ref, f32[512,128]{1,0:T(8,128)} %get-tuple-element.330.out_ref), custom_call_target="tpu_custom_call" | custom-call | tf_op jit(solution)/shard_map/pallas_call | solution.py:349
  121.0 0.0 copy-done.3
  121.0 5.5 %conditional.9 = (f32[1,3,1,1,102400]{4,3,2,1,0:T(1,128)}) conditional(s32[]{:T(128)} %convert_element_type.31, (f32[3,800,128]{2,1,0:T(8,128)S(1)}, f32[3,800,128]{2,1,0:T(8,128)S(1)}, f32[2,800,128]{2,1,0:T(8,128)S(1)}, s32[800,128]{1,0:T(8,128)}, f32[3,104,128]{2,1,0:T(8,128)}, /*index=5*/f32[3,104,128]{2,1,0:T(8,128)}, ...), branch_computations={%region_14.15_spmd, %region_15.16_spmd} | conditional | bytes 8 | solution.py:439
  121.0 5.5 %branch_0_fun.9 = (f32[3,800,128]{2,1,0:T(8,128)}, f32[512,128]{1,0:T(8,128)}, f32[3,8,896]{2,1,0:T(8,128)}) custom-call(f32[3,800,128]{2,1,0:T(8,128)S(1)} %get-tuple-element.251.cur_ref, f32[3,800,128]{2,1,0:T(8,128)S(1)} %get-tuple-element.252.prev_ref, f32[2,800,128]{2,1,0:T(8,128)S(1)} %get-tuple-element.253.coef_ref, ...), custom_call_target="tpu_custom_call" | custom-call | tf_op jit(solution)/shard_map/cond/branch_0_fun/pallas_call | solution.py:206
  (7 shorter events, 0.1 us)
Async XLA Ops:
  0.0 8.0 %copy-start = (f32[1,3,1,1,102400]{4,3,2,1,0:T(1,128)S(1)}, f32[1,3,1,1,102400]{4,3,2,1,0:T(1,128)}, u32[]{:S(2)}) copy-start(f32[1,3,1,1,102400]{4,3,2,1,0:T(1,128)} %param.17) | copy-start | bytes 3686404
  11.5 31.7 %copy-start.1 = (f32[1,2,1,1,102400]{4,3,2,1,0:T(1,128)S(1)}, f32[1,2,1,1,102400]{4,3,2,1,0:T(1,128)}, u32[]{:S(2)}) copy-start(f32[1,2,1,1,102400]{4,3,2,1,0:T(1,128)} %param.19) | copy-start | bytes 2457604
  74.8 20.2 %copy-start.2 = (f32[3,800,128]{2,1,0:T(8,128)S(1)}, f32[3,800,128]{2,1,0:T(8,128)}, u32[]{:S(2)}) copy-start(f32[3,800,128]{2,1,0:T(8,128)} %get-tuple-element.320.cur_ref) | copy-start | bytes 3686404
  100.8 20.2 %copy-start.3 = (f32[3,800,128]{2,1,0:T(8,128)S(1)}, f32[3,800,128]{2,1,0:T(8,128)}, u32[]{:S(2)}) copy-start(f32[3,800,128]{2,1,0:T(8,128)} %get-tuple-element.328.cur_ref) | copy-start | bytes 3686404

commit v8 on v7

--- a/solution.py
+++ b/solution.py
@@ -172,12 +172,12 @@
     total = jnp.zeros((REFINE * CX, CY), jnp.float32)
     for cb in range(REFINE):
         total = total + select_dot(field_ref[0, pl.ds(cb, REFINE * CX, stride=REFINE), :], spread(cb).T)
-    tiles_ref[...] = exact_dot(pick_ref[...], total / REFINE)
+    tiles_ref[...] = select_dot(pick_ref[...], total / REFINE)
 
 
 def elastic_tiles(field_ref, pick_ref, tiles_ref):
     uplift = field_ref[2, pl.ds(0, CX, stride=NL), :]
-    tiles_ref[...] = exact_dot(pick_ref[:, :CX], uplift)
+    tiles_ref[...] = select_dot(pick_ref[:, :CX], uplift)
 
 
 def prepare_kernel(tiles_of, cur_ref, pick_ref, tiles_ref, edges_ref):

time: 127 us -> 127 us (level)
  no operation moved by 1% of the time
where the time goes in v8:
time: 127 us; the launch traced here: 126 us
  Pallas kernels  114 us (90%)
  local copies, waits for them, and re-layouts  7.76 us (6%)
  other arithmetic  3.95 us (3%)
    pallas_call x4, Pallas kernels, exchange(): pl.pallas_call(functools.partial(exchange_kernel, (owners, rows_of, colum...  89.6 us
    pallas_call x4, Pallas kernels, run_step(): pl.pallas_call(kernel, out_shape=(jax.ShapeDtypeStruct((3, ROWS, CY), jnp...  22.3 us

profile of v8, /device:TPU:31, one launch (start us, length us, event | category | flops | bytes accessed | tf_op | source)
XLA Modules:
  0.0 126.3 jit_solution(9751878005726887286)
XLA Ops:
  0.0 0.0 copy-start
  0.0 0.8 fusion.12
  0.8 0.8 copy.12
  1.6 0.2 fusion.1
  1.9 0.9 fusion.3
  2.8 0.7 compare_select_fusion
  3.4 1.4 %scatter_custom_fusion.2 = s32[512]{0:T(512)S(1)} fusion(s32[256]{0:T(256)S(1)} %bitcast.71, s32[256]{0:T(256)S(1)} %bitcast.75, s32[]{:T(128)} %constant.9.clone.1), kind=kCustom, calls=%fused_computation.19 | custom fusion | bytes 2052 | tf_op jit(solution)/shard_map/scatter | solution.py:401
  4.9 1.4 %scatter_custom_fusion = s32[512]{0:T(512)S(1)} fusion(s32[256]{0:T(256)S(1)} %bitcast.72, s32[256]{0:T(256)S(1)} %bitcast.74, s32[]{:T(128)} %constant.10.clone.1), kind=kCustom, calls=%fused_computation.23 | custom fusion | bytes 2052 | tf_op jit(solution)/shard_map/scatter | solution.py:402
  6.3 1.6 %scatter_custom_fusion.1 = f32[512]{0:T(512)S(1)} fusion(s32[256]{0:T(256)S(1)} %bitcast.73, f32[256]{0:T(256)} %bitcast.78, f32[]{:T(128)} %constant.22.clone.1), kind=kCustom, calls=%fused_computation.21 | custom fusion | bytes 2560 | tf_op jit(solution)/shard_map/scatter | solution.py:403
  7.8 0.2 fusion
  8.0 0.0 copy-done
  8.0 0.1 broadcast_in_dim.38
  8.2 2.3 %conditional.5 = ((f32[512,128]{1,0:T(8,128)S(1)}, f32[3,8,896]{2,1,0:T(8,128)S(1)})) conditional(s32[]{:T(128)} %convert_element_type.31, (f32[3,800,128]{2,1,0:T(8,128)S(1)}, f32[512,80]{1,0:T(8,128)S(1)}) %tuple.67, (f32[3,800,128]{2,1,0:T(8,128)S(1)}, f32[512,80]{1,0:T(8,128)S(1)}) %tuple.68), branch_computations={%region_5.6_spmd, %region_6.7_spmd} | conditional | bytes 8 | solution.py:405
  8.2 2.2 %branch_0_fun.5 = (f32[512,128]{1,0:T(8,128)S(1)}, f32[3,8,896]{2,1,0:T(8,128)S(1)}) custom-call(f32[3,800,128]{2,1,0:T(8,128)S(1)} %get-tuple-element.184.cur_ref, f32[512,80]{1,0:T(8,128)S(1)} %get-tuple-element.185.pick_ref), custom_call_target="tpu_custom_call" | custom-call | tf_op jit(solution)/shard_map/cond/branch_0_fun/pallas_call | solution.py:189
  10.4 0.8 pad_maximum_fusion.out_ref
  11.3 0.0 copy-start.1
  11.3 29.0 %shard_map.75 = (f32[512,256]{1,0:T(8,128)}, f32[3,104,128]{2,1,0:T(8,128)}, f32[3,104,128]{2,1,0:T(8,128)}, f32[3,8,896]{2,1,0:T(8,128)}, f32[3,8,896]{2,1,0:T(8,128)}) custom-call(f32[3,800,128]{2,1,0:T(8,128)S(1)} %bitcast.37, f32[3,8,896]{2,1,0:T(8,128)S(1)} %get-tuple-element.305.edges_ref, f32[512,256]{1,0:T(8,128)} %pad_maximum_fusion.out_ref), custom_call_target="tpu_custom_call" | custom-call | tf_op jit(solution)/shard_map/pallas_call | solution.py:349
  40.2 1.1 convert_reduce_fusion
  41.3 1.7 %slice.23 = f32[512,128]{1,0:T(8,128)} slice(f32[512,256]{1,0:T(8,128)} %get-tuple-element.311), slice={[0:512], [0:128]} | slice | bytes 524288 | tf_op jit(solution)/shard_map/slice | solution.py:418
  43.0 0.0 copy-done.1
  43.0 5.8 %conditional.6 = ((f32[3,800,128]{2,1,0:T(8,128)S(1)}, f32[512,128]{1,0:T(8,128)}, f32[3,8,896]{2,1,0:T(8,128)})) conditional(s32[]{:T(128)} %convert_element_type.31, (f32[3,800,128]{2,1,0:T(8,128)S(1)}, f32[3,800,128]{2,1,0:T(8,128)}, f32[2,800,128]{2,1,0:T(8,128)S(1)}, s32[800,128]{1,0:T(8,128)}, f32[3,104,128]{2,1,0:T(8,128)}, ...), branch_computations={%region_8.9_spmd, %region_9.10_spmd} | conditional | bytes 8 | solution.py:439
  43.0 5.8 %branch_0_fun.6 = (f32[3,800,128]{2,1,0:T(8,128)S(1)}, f32[512,128]{1,0:T(8,128)}, f32[3,8,896]{2,1,0:T(8,128)}) custom-call(f32[3,800,128]{2,1,0:T(8,128)S(1)} %get-tuple-element.188.cur_ref, f32[3,800,128]{2,1,0:T(8,128)} %get-tuple-element.189.prev_ref, f32[2,800,128]{2,1,0:T(8,128)S(1)} %get-tuple-element.190.coef_ref, ...), custom_call_target="tpu_custom_call" | custom-call | tf_op jit(solution)/shard_map/cond/branch_0_fun/pallas_call | solution.py:206
  48.9 20.2 %shard_map.76 = (f32[512,128]{1,0:T(8,128)}, f32[3,104,128]{2,1,0:T(8,128)}, f32[3,104,128]{2,1,0:T(8,128)}, f32[3,8,896]{2,1,0:T(8,128)}, f32[3,8,896]{2,1,0:T(8,128)}) custom-call(f32[3,800,128]{2,1,0:T(8,128)S(1)} %get-tuple-element.312.cur_ref, f32[3,8,896]{2,1,0:T(8,128)} %get-tuple-element.313.edges_ref, f32[512,128]{1,0:T(8,128)} %get-tuple-element.314.out_ref), custom_call_target="tpu_custom_call" | custom-call | tf_op jit(solution)/shard_map/pallas_call | solution.py:349
  69.1 5.5 %conditional.7 = ((f32[3,800,128]{2,1,0:T(8,128)}, f32[512,128]{1,0:T(8,128)}, f32[3,8,896]{2,1,0:T(8,128)})) conditional(s32[]{:T(128)} %convert_element_type.31, (f32[3,800,128]{2,1,0:T(8,128)S(1)}, f32[3,800,128]{2,1,0:T(8,128)S(1)}, f32[2,800,128]{2,1,0:T(8,128)S(1)}, s32[800,128]{1,0:T(8,128)}, f32[3,104,128]{2,1,0:T(8,128)}, ...), branch_computations={%region_10.11_spmd, %region_11.12_spmd} | conditional | bytes 8 | solution.py:439
  69.1 5.5 %branch_0_fun.7 = (f32[3,800,128]{2,1,0:T(8,128)}, f32[512,128]{1,0:T(8,128)}, f32[3,8,896]{2,1,0:T(8,128)}) custom-call(f32[3,800,128]{2,1,0:T(8,128)S(1)} %get-tuple-element.209.cur_ref, f32[3,800,128]{2,1,0:T(8,128)S(1)} %get-tuple-element.210.prev_ref, f32[2,800,128]{2,1,0:T(8,128)S(1)} %get-tuple-element.211.coef_ref, ...), custom_call_target="tpu_custom_call" | custom-call | tf_op jit(solution)/shard_map/cond/branch_0_fun/pallas_call | solution.py:206
  74.6 0.0 copy-start.2
  74.6 20.2 %shard_map.77 = (f32[512,128]{1,0:T(8,128)}, f32[3,104,128]{2,1,0:T(8,128)}, f32[3,104,128]{2,1,0:T(8,128)}, f32[3,8,896]{2,1,0:T(8,128)}, f32[3,8,896]{2,1,0:T(8,128)}) custom-call(f32[3,800,128]{2,1,0:T(8,128)} %get-tuple-element.320.cur_ref, f32[3,8,896]{2,1,0:T(8,128)} %get-tuple-element.321.edges_ref, f32[512,128]{1,0:T(8,128)} %get-tuple-element.322.out_ref), custom_call_target="tpu_custom_call" | custom-call | tf_op jit(solution)/shard_map/pallas_call | solution.py:349
  94.9 0.0 copy-done.2
  94.9 5.7 %conditional.8 = ((f32[3,800,128]{2,1,0:T(8,128)}, f32[512,128]{1,0:T(8,128)}, f32[3,8,896]{2,1,0:T(8,128)})) conditional(s32[]{:T(128)} %convert_element_type.31, (f32[3,800,128]{2,1,0:T(8,128)S(1)}, f32[3,800,128]{2,1,0:T(8,128)S(1)}, f32[2,800,128]{2,1,0:T(8,128)S(1)}, s32[800,128]{1,0:T(8,128)}, f32[3,104,128]{2,1,0:T(8,128)}, ...), branch_computations={%region_12.13_spmd, %region_13.14_spmd} | conditional | bytes 8 | solution.py:439
  95.1 5.5 %branch_0_fun.8 = (f32[3,800,128]{2,1,0:T(8,128)}, f32[512,128]{1,0:T(8,128)}, f32[3,8,896]{2,1,0:T(8,128)}) custom-call(f32[3,800,128]{2,1,0:T(8,128)S(1)} %get-tuple-element.230.cur_ref, f32[3,800,128]{2,1,0:T(8,128)S(1)} %get-tuple-element.231.prev_ref, f32[2,800,128]{2,1,0:T(8,128)S(1)} %get-tuple-element.232.coef_ref, ...), custom_call_target="tpu_custom_call" | custom-call | tf_op jit(solution)/shard_map/cond/branch_0_fun/pallas_call | solution.py:206
  100.6 0.0 copy-start.3
  100.6 20.1 %shard_map.78 = (f32[512,128]{1,0:T(8,128)}, f32[3,104,128]{2,1,0:T(8,128)}, f32[3,104,128]{2,1,0:T(8,128)}, f32[3,8,896]{2,1,0:T(8,128)}, f32[3,8,896]{2,1,0:T(8,128)}) custom-call(f32[3,800,128]{2,1,0:T(8,128)} %get-tuple-element.328.cur_ref, f32[3,8,896]{2,1,0:T(8,128)} %get-tuple-element.329.edges_ref, f32[512,128]{1,0:T(8,128)} %get-tuple-element.330.out_ref), custom_call_target="tpu_custom_call" | custom-call | tf_op jit(solution)/shard_map/pallas_call | solution.py:349
  120.8 0.0 copy-done.3
  120.8 5.5 %conditional.9 = (f32[1,3,1,1,102400]{4,3,2,1,0:T(1,128)}) conditional(s32[]{:T(128)} %convert_element_type.31, (f32[3,800,128]{2,1,0:T(8,128)S(1)}, f32[3,800,128]{2,1,0:T(8,128)S(1)}, f32[2,800,128]{2,1,0:T(8,128)S(1)}, s32[800,128]{1,0:T(8,128)}, f32[3,104,128]{2,1,0:T(8,128)}, /*index=5*/f32[3,104,128]{2,1,0:T(8,128)}, ...), branch_computations={%region_14.15_spmd, %region_15.16_spmd} | conditional | bytes 8 | solution.py:439
  120.8 5.5 %branch_0_fun.9 = (f32[3,800,128]{2,1,0:T(8,128)}, f32[512,128]{1,0:T(8,128)}, f32[3,8,896]{2,1,0:T(8,128)}) custom-call(f32[3,800,128]{2,1,0:T(8,128)S(1)} %get-tuple-element.251.cur_ref, f32[3,800,128]{2,1,0:T(8,128)S(1)} %get-tuple-element.252.prev_ref, f32[2,800,128]{2,1,0:T(8,128)S(1)} %get-tuple-element.253.coef_ref, ...), custom_call_target="tpu_custom_call" | custom-call | tf_op jit(solution)/shard_map/cond/branch_0_fun/pallas_call | solution.py:206
  (7 shorter events, 0.1 us)
Async XLA Ops:
  0.0 8.0 %copy-start = (f32[1,3,1,1,102400]{4,3,2,1,0:T(1,128)S(1)}, f32[1,3,1,1,102400]{4,3,2,1,0:T(1,128)}, u32[]{:S(2)}) copy-start(f32[1,3,1,1,102400]{4,3,2,1,0:T(1,128)} %param.17) | copy-start | bytes 3686404
  11.3 31.7 %copy-start.1 = (f32[1,2,1,1,102400]{4,3,2,1,0:T(1,128)S(1)}, f32[1,2,1,1,102400]{4,3,2,1,0:T(1,128)}, u32[]{:S(2)}) copy-start(f32[1,2,1,1,102400]{4,3,2,1,0:T(1,128)} %param.19) | copy-start | bytes 2457604
  74.6 20.2 %copy-start.2 = (f32[3,800,128]{2,1,0:T(8,128)S(1)}, f32[3,800,128]{2,1,0:T(8,128)}, u32[]{:S(2)}) copy-start(f32[3,800,128]{2,1,0:T(8,128)} %get-tuple-element.320.cur_ref) | copy-start | bytes 3686404
  100.6 20.2 %copy-start.3 = (f32[3,800,128]{2,1,0:T(8,128)S(1)}, f32[3,800,128]{2,1,0:T(8,128)}, u32[]{:S(2)}) copy-start(f32[3,800,128]{2,1,0:T(8,128)} %get-tuple-element.328.cur_ref) | copy-start | bytes 3686404

commit v9 on v7

--- a/solution.py
+++ b/solution.py
@@ -79,8 +79,8 @@
         edges_ref[f, :, pl.ds(0, ROWS)] = picked
 
 
-def fill_sides(low_rows_ref, high_rows_ref, left_pad, right_pad):
-    for f in range(3):
+def fill_sides(low_rows_ref, high_rows_ref, left_pad, right_pad, fields=(0, 1, 2)):
+    for f in fields:
         left_pad[f, pl.ds(EDGE, ROWS), :] = jnp.transpose(low_rows_ref[f])[:ROWS, 0:1]
         right_pad[f, pl.ds(EDGE, ROWS), :] = jnp.transpose(high_rows_ref[f])[:ROWS, 1:2]
 
@@ -128,7 +128,7 @@
 def shallow_kernel(cur_ref, prev_ref, coef_ref, wet_ref, low_ref, high_ref, low_rows_ref, high_rows_ref, rows_ref,
                    arrived_ref, pick_ref, out_ref, tiles_ref, edges_ref, scratch, source_ref, left_pad, right_pad):
     fill_scratch(scratch, cur_ref, low_ref, high_ref, 3)
-    fill_sides(low_rows_ref, high_rows_ref, left_pad, right_pad)
+    fill_sides(low_rows_ref, high_rows_ref, left_pad, right_pad, (0, 2))
     coarse_source = landing_sum(rows_ref, arrived_ref, REFINE * CX)
     for cb in range(REFINE):
         source_ref[pl.ds(cb, REFINE * CX, stride=REFINE), :] = select_dot(coarse_source, spread(cb))

time: 127 us -> 127 us (level)
  no operation moved by 1% of the time
where the time goes in v9:
time: 127 us
  Pallas kernels  114 us (90%)
  local copies, waits for them, and re-layouts  7.76 us (6%)
  other arithmetic  3.96 us (3%)
    pallas_call x4, Pallas kernels, exchange(): pl.pallas_call(functools.partial(exchange_kernel, (owners, rows_of, colum...  89.6 us
    pallas_call x4, Pallas kernels, run_step(): pl.pallas_call(kernel, out_shape=(jax.ShapeDtypeStruct((3, ROWS, CY), jnp...  22.5 us

profile of v9, /device:TPU:31, one launch (start us, length us, event | category | flops | bytes accessed | tf_op | source)
XLA Modules:
  0.0 126.6 jit_solution(5516641150085266052)
XLA Ops:
  0.0 0.0 copy-start
  0.0 0.8 fusion.12
  0.8 0.8 copy.12
  1.6 0.2 fusion.1
  1.9 0.9 fusion.3
  2.8 0.7 compare_select_fusion
  3.4 1.4 %scatter_custom_fusion.2 = s32[512]{0:T(512)S(1)} fusion(s32[256]{0:T(256)S(1)} %bitcast.71, s32[256]{0:T(256)S(1)} %bitcast.75, s32[]{:T(128)} %constant.9.clone.1), kind=kCustom, calls=%fused_computation.19 | custom fusion | bytes 2052 | tf_op jit(solution)/shard_map/scatter | solution.py:401
  4.9 1.4 %scatter_custom_fusion = s32[512]{0:T(512)S(1)} fusion(s32[256]{0:T(256)S(1)} %bitcast.72, s32[256]{0:T(256)S(1)} %bitcast.74, s32[]{:T(128)} %constant.10.clone.1), kind=kCustom, calls=%fused_computation.23 | custom fusion | bytes 2052 | tf_op jit(solution)/shard_map/scatter | solution.py:402
  6.3 1.6 %scatter_custom_fusion.1 = f32[512]{0:T(512)S(1)} fusion(s32[256]{0:T(256)S(1)} %bitcast.73, f32[256]{0:T(256)} %bitcast.78, f32[]{:T(128)} %constant.22.clone.1), kind=kCustom, calls=%fused_computation.21 | custom fusion | bytes 2560 | tf_op jit(solution)/shard_map/scatter | solution.py:403
  7.8 0.2 fusion
  8.0 0.0 copy-done
  8.0 0.1 broadcast_in_dim.38
  8.2 2.4 %conditional.5 = ((f32[512,128]{1,0:T(8,128)S(1)}, f32[3,8,896]{2,1,0:T(8,128)S(1)})) conditional(s32[]{:T(128)} %convert_element_type.31, (f32[3,800,128]{2,1,0:T(8,128)S(1)}, f32[512,80]{1,0:T(8,128)S(1)}) %tuple.67, (f32[3,800,128]{2,1,0:T(8,128)S(1)}, f32[512,80]{1,0:T(8,128)S(1)}) %tuple.68), branch_computations={%region_5.6_spmd, %region_6.7_spmd} | conditional | bytes 8 | solution.py:405
  8.2 2.4 %branch_0_fun.5 = (f32[512,128]{1,0:T(8,128)S(1)}, f32[3,8,896]{2,1,0:T(8,128)S(1)}) custom-call(f32[3,800,128]{2,1,0:T(8,128)S(1)} %get-tuple-element.184.cur_ref, f32[512,80]{1,0:T(8,128)S(1)} %get-tuple-element.185.pick_ref), custom_call_target="tpu_custom_call" | custom-call | tf_op jit(solution)/shard_map/cond/branch_0_fun/pallas_call | solution.py:189
  10.6 0.9 pad_maximum_fusion.out_ref
  11.5 0.0 copy-start.1
  11.5 29.0 %shard_map.75 = (f32[512,256]{1,0:T(8,128)}, f32[3,104,128]{2,1,0:T(8,128)}, f32[3,104,128]{2,1,0:T(8,128)}, f32[3,8,896]{2,1,0:T(8,128)}, f32[3,8,896]{2,1,0:T(8,128)}) custom-call(f32[3,800,128]{2,1,0:T(8,128)S(1)} %bitcast.37, f32[3,8,896]{2,1,0:T(8,128)S(1)} %get-tuple-element.305.edges_ref, f32[512,256]{1,0:T(8,128)} %pad_maximum_fusion.out_ref), custom_call_target="tpu_custom_call" | custom-call | tf_op jit(solution)/shard_map/pallas_call | solution.py:349
  40.4 1.1 convert_reduce_fusion
  41.5 1.7 %slice.23 = f32[512,128]{1,0:T(8,128)} slice(f32[512,256]{1,0:T(8,128)} %get-tuple-element.311), slice={[0:512], [0:128]} | slice | bytes 524288 | tf_op jit(solution)/shard_map/slice | solution.py:418
  43.2 0.0 copy-done.1
  43.2 5.9 %conditional.6 = ((f32[3,800,128]{2,1,0:T(8,128)S(1)}, f32[512,128]{1,0:T(8,128)}, f32[3,8,896]{2,1,0:T(8,128)})) conditional(s32[]{:T(128)} %convert_element_type.31, (f32[3,800,128]{2,1,0:T(8,128)S(1)}, f32[3,800,128]{2,1,0:T(8,128)}, f32[2,800,128]{2,1,0:T(8,128)S(1)}, s32[800,128]{1,0:T(8,128)}, f32[3,104,128]{2,1,0:T(8,128)}, ...), branch_computations={%region_8.9_spmd, %region_9.10_spmd} | conditional | bytes 8 | solution.py:439
  43.2 5.9 %branch_0_fun.6 = (f32[3,800,128]{2,1,0:T(8,128)S(1)}, f32[512,128]{1,0:T(8,128)}, f32[3,8,896]{2,1,0:T(8,128)}) custom-call(f32[3,800,128]{2,1,0:T(8,128)S(1)} %get-tuple-element.188.cur_ref, f32[3,800,128]{2,1,0:T(8,128)} %get-tuple-element.189.prev_ref, f32[2,800,128]{2,1,0:T(8,128)S(1)} %get-tuple-element.190.coef_ref, ...), custom_call_target="tpu_custom_call" | custom-call | tf_op jit(solution)/shard_map/cond/branch_0_fun/pallas_call | solution.py:206
  49.1 20.2 %shard_map.76 = (f32[512,128]{1,0:T(8,128)}, f32[3,104,128]{2,1,0:T(8,128)}, f32[3,104,128]{2,1,0:T(8,128)}, f32[3,8,896]{2,1,0:T(8,128)}, f32[3,8,896]{2,1,0:T(8,128)}) custom-call(f32[3,800,128]{2,1,0:T(8,128)S(1)} %get-tuple-element.312.cur_ref, f32[3,8,896]{2,1,0:T(8,128)} %get-tuple-element.313.edges_ref, f32[512,128]{1,0:T(8,128)} %get-tuple-element.314.out_ref), custom_call_target="tpu_custom_call" | custom-call | tf_op jit(solution)/shard_map/pallas_call | solution.py:349
  69.3 5.6 %conditional.7 = ((f32[3,800,128]{2,1,0:T(8,128)}, f32[512,128]{1,0:T(8,128)}, f32[3,8,896]{2,1,0:T(8,128)})) conditional(s32[]{:T(128)} %convert_element_type.31, (f32[3,800,128]{2,1,0:T(8,128)S(1)}, f32[3,800,128]{2,1,0:T(8,128)S(1)}, f32[2,800,128]{2,1,0:T(8,128)S(1)}, s32[800,128]{1,0:T(8,128)}, f32[3,104,128]{2,1,0:T(8,128)}, ...), branch_computations={%region_10.11_spmd, %region_11.12_spmd} | conditional | bytes 8 | solution.py:439
  69.3 5.5 %branch_0_fun.7 = (f32[3,800,128]{2,1,0:T(8,128)}, f32[512,128]{1,0:T(8,128)}, f32[3,8,896]{2,1,0:T(8,128)}) custom-call(f32[3,800,128]{2,1,0:T(8,128)S(1)} %get-tuple-element.209.cur_ref, f32[3,800,128]{2,1,0:T(8,128)S(1)} %get-tuple-element.210.prev_ref, f32[2,800,128]{2,1,0:T(8,128)S(1)} %get-tuple-element.211.coef_ref, ...), custom_call_target="tpu_custom_call" | custom-call | tf_op jit(solution)/shard_map/cond/branch_0_fun/pallas_call | solution.py:206
  74.9 0.0 copy-start.2
  74.9 20.2 %shard_map.77 = (f32[512,128]{1,0:T(8,128)}, f32[3,104,128]{2,1,0:T(8,128)}, f32[3,104,128]{2,1,0:T(8,128)}, f32[3,8,896]{2,1,0:T(8,128)}, f32[3,8,896]{2,1,0:T(8,128)}) custom-call(f32[3,800,128]{2,1,0:T(8,128)} %get-tuple-element.320.cur_ref, f32[3,8,896]{2,1,0:T(8,128)} %get-tuple-element.321.edges_ref, f32[512,128]{1,0:T(8,128)} %get-tuple-element.322.out_ref), custom_call_target="tpu_custom_call" | custom-call | tf_op jit(solution)/shard_map/pallas_call | solution.py:349
  95.1 0.0 copy-done.2
  95.1 5.8 %conditional.8 = ((f32[3,800,128]{2,1,0:T(8,128)}, f32[512,128]{1,0:T(8,128)}, f32[3,8,896]{2,1,0:T(8,128)})) conditional(s32[]{:T(128)} %convert_element_type.31, (f32[3,800,128]{2,1,0:T(8,128)S(1)}, f32[3,800,128]{2,1,0:T(8,128)S(1)}, f32[2,800,128]{2,1,0:T(8,128)S(1)}, s32[800,128]{1,0:T(8,128)}, f32[3,104,128]{2,1,0:T(8,128)}, ...), branch_computations={%region_12.13_spmd, %region_13.14_spmd} | conditional | bytes 8 | solution.py:439
  95.4 5.5 %branch_0_fun.8 = (f32[3,800,128]{2,1,0:T(8,128)}, f32[512,128]{1,0:T(8,128)}, f32[3,8,896]{2,1,0:T(8,128)}) custom-call(f32[3,800,128]{2,1,0:T(8,128)S(1)} %get-tuple-element.230.cur_ref, f32[3,800,128]{2,1,0:T(8,128)S(1)} %get-tuple-element.231.prev_ref, f32[2,800,128]{2,1,0:T(8,128)S(1)} %get-tuple-element.232.coef_ref, ...), custom_call_target="tpu_custom_call" | custom-call | tf_op jit(solution)/shard_map/cond/branch_0_fun/pallas_call | solution.py:206
  100.9 0.0 copy-start.3
  100.9 20.1 %shard_map.78 = (f32[512,128]{1,0:T(8,128)}, f32[3,104,128]{2,1,0:T(8,128)}, f32[3,104,128]{2,1,0:T(8,128)}, f32[3,8,896]{2,1,0:T(8,128)}, f32[3,8,896]{2,1,0:T(8,128)}) custom-call(f32[3,800,128]{2,1,0:T(8,128)} %get-tuple-element.328.cur_ref, f32[3,8,896]{2,1,0:T(8,128)} %get-tuple-element.329.edges_ref, f32[512,128]{1,0:T(8,128)} %get-tuple-element.330.out_ref), custom_call_target="tpu_custom_call" | custom-call | tf_op jit(solution)/shard_map/pallas_call | solution.py:349
  121.1 0.0 copy-done.3
  121.1 5.6 %conditional.9 = (f32[1,3,1,1,102400]{4,3,2,1,0:T(1,128)}) conditional(s32[]{:T(128)} %convert_element_type.31, (f32[3,800,128]{2,1,0:T(8,128)S(1)}, f32[3,800,128]{2,1,0:T(8,128)S(1)}, f32[2,800,128]{2,1,0:T(8,128)S(1)}, s32[800,128]{1,0:T(8,128)}, f32[3,104,128]{2,1,0:T(8,128)}, /*index=5*/f32[3,104,128]{2,1,0:T(8,128)}, ...), branch_computations={%region_14.15_spmd, %region_15.16_spmd} | conditional | bytes 8 | solution.py:439
  121.1 5.5 %branch_0_fun.9 = (f32[3,800,128]{2,1,0:T(8,128)}, f32[512,128]{1,0:T(8,128)}, f32[3,8,896]{2,1,0:T(8,128)}) custom-call(f32[3,800,128]{2,1,0:T(8,128)S(1)} %get-tuple-element.251.cur_ref, f32[3,800,128]{2,1,0:T(8,128)S(1)} %get-tuple-element.252.prev_ref, f32[2,800,128]{2,1,0:T(8,128)S(1)} %get-tuple-element.253.coef_ref, ...), custom_call_target="tpu_custom_call" | custom-call | tf_op jit(solution)/shard_map/cond/branch_0_fun/pallas_call | solution.py:206
  (7 shorter events, 0.1 us)
Async XLA Ops:
  0.0 8.0 %copy-start = (f32[1,3,1,1,102400]{4,3,2,1,0:T(1,128)S(1)}, f32[1,3,1,1,102400]{4,3,2,1,0:T(1,128)}, u32[]{:S(2)}) copy-start(f32[1,3,1,1,102400]{4,3,2,1,0:T(1,128)} %param.17) | copy-start | bytes 3686404
  11.5 31.7 %copy-start.1 = (f32[1,2,1,1,102400]{4,3,2,1,0:T(1,128)S(1)}, f32[1,2,1,1,102400]{4,3,2,1,0:T(1,128)}, u32[]{:S(2)}) copy-start(f32[1,2,1,1,102400]{4,3,2,1,0:T(1,128)} %param.19) | copy-start | bytes 2457604
  74.9 20.2 %copy-start.2 = (f32[3,800,128]{2,1,0:T(8,128)S(1)}, f32[3,800,128]{2,1,0:T(8,128)}, u32[]{:S(2)}) copy-start(f32[3,800,128]{2,1,0:T(8,128)} %get-tuple-element.320.cur_ref) | copy-start | bytes 3686404
  100.9 20.2 %copy-start.3 = (f32[3,800,128]{2,1,0:T(8,128)S(1)}, f32[3,800,128]{2,1,0:T(8,128)}, u32[]{:S(2)}) copy-start(f32[3,800,128]{2,1,0:T(8,128)} %get-tuple-element.328.cur_ref) | copy-start | bytes 3686404

commit v10 on v9

--- a/solution.py
+++ b/solution.py
@@ -68,14 +68,16 @@
     return exact_dot(one_hot, arrived_ref[...])
 
 
-def edge_rows(out_ref, edges_ref):
+def edge_rows(out_ref, edges_ref, fields=(0, 1, 2)):
     rows = lax.broadcasted_iota(jnp.int32, (8, CY), 0)
     lanes = lax.broadcasted_iota(jnp.int32, (8, CY), 1)
     select = (((rows == 0) & (lanes == CY - 1)) | ((rows == 1) & (lanes == 0))).astype(jnp.float32)
     for f in range(3):
+        edges_ref[f] = jnp.zeros(edges_ref.shape[1:], jnp.float32)
+        if f not in fields:
+            continue
         picked = lax.dot_general(select, out_ref[f], (((1,), (1,)), ((), ())), precision=lax.Precision.HIGH,
                                  preferred_element_type=jnp.float32)
-        edges_ref[f] = jnp.zeros(edges_ref.shape[1:], jnp.float32)
         edges_ref[f, :, pl.ds(0, ROWS)] = picked
 
 
@@ -165,7 +167,7 @@
             prev_ref[0, pl.ds(r0, CHUNK), :] - area * divergence + source_ref[pl.ds(r0, CHUNK), :]
         )
     shallow_tiles(out_ref, pick_ref, tiles_ref)
-    edge_rows(out_ref, edges_ref)
+    edge_rows(out_ref, edges_ref, (0, 2))
 
 
 def shallow_tiles(field_ref, pick_ref, tiles_ref):

time: 127 us -> 126 us (level)
  no operation moved by 1% of the time
where the time goes in v10:
time: 126 us
  Pallas kernels  114 us (90%)
  local copies, waits for them, and re-layouts  7.76 us (6%)
  other arithmetic  3.96 us (3%)
    pallas_call x4, Pallas kernels, exchange(): pl.pallas_call(functools.partial(exchange_kernel, (owners, rows_of, colum...  89.6 us
    pallas_call x4, Pallas kernels, run_step(): pl.pallas_call(kernel, out_shape=(jax.ShapeDtypeStruct((3, ROWS, CY), jnp...  21.5 us

profile of v10, /device:TPU:31, one launch (start us, length us, event | category | flops | bytes accessed | tf_op | source)
XLA Modules:
  0.0 125.7 jit_solution(17017792464206131153)
XLA Ops:
  0.0 0.0 copy-start
  0.0 0.8 fusion.12
  0.8 0.8 copy.12
  1.6 0.2 fusion.1
  1.9 0.9 fusion.3
  2.8 0.7 compare_select_fusion
  3.4 1.4 %scatter_custom_fusion.2 = s32[512]{0:T(512)S(1)} fusion(s32[256]{0:T(256)S(1)} %bitcast.71, s32[256]{0:T(256)S(1)} %bitcast.75, s32[]{:T(128)} %constant.9.clone.1), kind=kCustom, calls=%fused_computation.19 | custom fusion | bytes 2052 | tf_op jit(solution)/shard_map/scatter | solution.py:403
  4.9 1.4 %scatter_custom_fusion = s32[512]{0:T(512)S(1)} fusion(s32[256]{0:T(256)S(1)} %bitcast.72, s32[256]{0:T(256)S(1)} %bitcast.74, s32[]{:T(128)} %constant.10.clone.1), kind=kCustom, calls=%fused_computation.23 | custom fusion | bytes 2052 | tf_op jit(solution)/shard_map/scatter | solution.py:404
  6.3 1.6 %scatter_custom_fusion.1 = f32[512]{0:T(512)S(1)} fusion(s32[256]{0:T(256)S(1)} %bitcast.73, f32[256]{0:T(256)} %bitcast.78, f32[]{:T(128)} %constant.22.clone.1), kind=kCustom, calls=%fused_computation.21 | custom fusion | bytes 2560 | tf_op jit(solution)/shard_map/scatter | solution.py:405
  7.8 0.2 fusion
  8.0 0.0 copy-done
  8.0 0.1 broadcast_in_dim.38
  8.2 2.4 %conditional.5 = ((f32[512,128]{1,0:T(8,128)S(1)}, f32[3,8,896]{2,1,0:T(8,128)S(1)})) conditional(s32[]{:T(128)} %convert_element_type.31, (f32[3,800,128]{2,1,0:T(8,128)S(1)}, f32[512,80]{1,0:T(8,128)S(1)}) %tuple.67, (f32[3,800,128]{2,1,0:T(8,128)S(1)}, f32[512,80]{1,0:T(8,128)S(1)}) %tuple.68), branch_computations={%region_5.6_spmd, %region_6.7_spmd} | conditional | bytes 8 | solution.py:407
  8.2 2.4 %branch_0_fun.5 = (f32[512,128]{1,0:T(8,128)S(1)}, f32[3,8,896]{2,1,0:T(8,128)S(1)}) custom-call(f32[3,800,128]{2,1,0:T(8,128)S(1)} %get-tuple-element.184.cur_ref, f32[512,80]{1,0:T(8,128)S(1)} %get-tuple-element.185.pick_ref), custom_call_target="tpu_custom_call" | custom-call | tf_op jit(solution)/shard_map/cond/branch_0_fun/pallas_call | solution.py:191
  10.6 0.9 pad_maximum_fusion.out_ref
  11.5 0.0 copy-start.1
  11.5 29.0 %shard_map.75 = (f32[512,256]{1,0:T(8,128)}, f32[3,104,128]{2,1,0:T(8,128)}, f32[3,104,128]{2,1,0:T(8,128)}, f32[3,8,896]{2,1,0:T(8,128)}, f32[3,8,896]{2,1,0:T(8,128)}) custom-call(f32[3,800,128]{2,1,0:T(8,128)S(1)} %bitcast.37, f32[3,8,896]{2,1,0:T(8,128)S(1)} %get-tuple-element.305.edges_ref, f32[512,256]{1,0:T(8,128)} %pad_maximum_fusion.out_ref), custom_call_target="tpu_custom_call" | custom-call | tf_op jit(solution)/shard_map/pallas_call | solution.py:351
  40.4 1.1 convert_reduce_fusion
  41.5 1.7 %slice.23 = f32[512,128]{1,0:T(8,128)} slice(f32[512,256]{1,0:T(8,128)} %get-tuple-element.311), slice={[0:512], [0:128]} | slice | bytes 524288 | tf_op jit(solution)/shard_map/slice | solution.py:420
  43.2 0.0 copy-done.1
  43.2 5.6 %conditional.6 = ((f32[3,800,128]{2,1,0:T(8,128)S(1)}, f32[512,128]{1,0:T(8,128)}, f32[3,8,896]{2,1,0:T(8,128)})) conditional(s32[]{:T(128)} %convert_element_type.31, (f32[3,800,128]{2,1,0:T(8,128)S(1)}, f32[3,800,128]{2,1,0:T(8,128)}, f32[2,800,128]{2,1,0:T(8,128)S(1)}, s32[800,128]{1,0:T(8,128)}, f32[3,104,128]{2,1,0:T(8,128)}, ...), branch_computations={%region_8.9_spmd, %region_9.10_spmd} | conditional | bytes 8 | solution.py:441
  43.2 5.6 %branch_0_fun.6 = (f32[3,800,128]{2,1,0:T(8,128)S(1)}, f32[512,128]{1,0:T(8,128)}, f32[3,8,896]{2,1,0:T(8,128)}) custom-call(f32[3,800,128]{2,1,0:T(8,128)S(1)} %get-tuple-element.188.cur_ref, f32[3,800,128]{2,1,0:T(8,128)} %get-tuple-element.189.prev_ref, f32[2,800,128]{2,1,0:T(8,128)S(1)} %get-tuple-element.190.coef_ref, ...), custom_call_target="tpu_custom_call" | custom-call | tf_op jit(solution)/shard_map/cond/branch_0_fun/pallas_call | solution.py:208
  48.8 20.2 %shard_map.76 = (f32[512,128]{1,0:T(8,128)}, f32[3,104,128]{2,1,0:T(8,128)}, f32[3,104,128]{2,1,0:T(8,128)}, f32[3,8,896]{2,1,0:T(8,128)}, f32[3,8,896]{2,1,0:T(8,128)}) custom-call(f32[3,800,128]{2,1,0:T(8,128)S(1)} %get-tuple-element.312.cur_ref, f32[3,8,896]{2,1,0:T(8,128)} %get-tuple-element.313.edges_ref, f32[512,128]{1,0:T(8,128)} %get-tuple-element.314.out_ref), custom_call_target="tpu_custom_call" | custom-call | tf_op jit(solution)/shard_map/pallas_call | solution.py:351
  69.1 5.3 %conditional.7 = ((f32[3,800,128]{2,1,0:T(8,128)}, f32[512,128]{1,0:T(8,128)}, f32[3,8,896]{2,1,0:T(8,128)})) conditional(s32[]{:T(128)} %convert_element_type.31, (f32[3,800,128]{2,1,0:T(8,128)S(1)}, f32[3,800,128]{2,1,0:T(8,128)S(1)}, f32[2,800,128]{2,1,0:T(8,128)S(1)}, s32[800,128]{1,0:T(8,128)}, f32[3,104,128]{2,1,0:T(8,128)}, ...), branch_computations={%region_10.11_spmd, %region_11.12_spmd} | conditional | bytes 8 | solution.py:441
  69.1 5.3 %branch_0_fun.7 = (f32[3,800,128]{2,1,0:T(8,128)}, f32[512,128]{1,0:T(8,128)}, f32[3,8,896]{2,1,0:T(8,128)}) custom-call(f32[3,800,128]{2,1,0:T(8,128)S(1)} %get-tuple-element.209.cur_ref, f32[3,800,128]{2,1,0:T(8,128)S(1)} %get-tuple-element.210.prev_ref, f32[2,800,128]{2,1,0:T(8,128)S(1)} %get-tuple-element.211.coef_ref, ...), custom_call_target="tpu_custom_call" | custom-call | tf_op jit(solution)/shard_map/cond/branch_0_fun/pallas_call | solution.py:208
  74.4 0.0 copy-start.2
  74.4 20.2 %shard_map.77 = (f32[512,128]{1,0:T(8,128)}, f32[3,104,128]{2,1,0:T(8,128)}, f32[3,104,128]{2,1,0:T(8,128)}, f32[3,8,896]{2,1,0:T(8,128)}, f32[3,8,896]{2,1,0:T(8,128)}) custom-call(f32[3,800,128]{2,1,0:T(8,128)} %get-tuple-element.320.cur_ref, f32[3,8,896]{2,1,0:T(8,128)} %get-tuple-element.321.edges_ref, f32[512,128]{1,0:T(8,128)} %get-tuple-element.322.out_ref), custom_call_target="tpu_custom_call" | custom-call | tf_op jit(solution)/shard_map/pallas_call | solution.py:351
  94.6 0.0 copy-done.2
  94.7 5.5 %conditional.8 = ((f32[3,800,128]{2,1,0:T(8,128)}, f32[512,128]{1,0:T(8,128)}, f32[3,8,896]{2,1,0:T(8,128)})) conditional(s32[]{:T(128)} %convert_element_type.31, (f32[3,800,128]{2,1,0:T(8,128)S(1)}, f32[3,800,128]{2,1,0:T(8,128)S(1)}, f32[2,800,128]{2,1,0:T(8,128)S(1)}, s32[800,128]{1,0:T(8,128)}, f32[3,104,128]{2,1,0:T(8,128)}, ...), branch_computations={%region_12.13_spmd, %region_13.14_spmd} | conditional | bytes 8 | solution.py:441
  94.9 5.3 %branch_0_fun.8 = (f32[3,800,128]{2,1,0:T(8,128)}, f32[512,128]{1,0:T(8,128)}, f32[3,8,896]{2,1,0:T(8,128)}) custom-call(f32[3,800,128]{2,1,0:T(8,128)S(1)} %get-tuple-element.230.cur_ref, f32[3,800,128]{2,1,0:T(8,128)S(1)} %get-tuple-element.231.prev_ref, f32[2,800,128]{2,1,0:T(8,128)S(1)} %get-tuple-element.232.coef_ref, ...), custom_call_target="tpu_custom_call" | custom-call | tf_op jit(solution)/shard_map/cond/branch_0_fun/pallas_call | solution.py:208
  100.2 0.0 copy-start.3
  100.2 20.1 %shard_map.78 = (f32[512,128]{1,0:T(8,128)}, f32[3,104,128]{2,1,0:T(8,128)}, f32[3,104,128]{2,1,0:T(8,128)}, f32[3,8,896]{2,1,0:T(8,128)}, f32[3,8,896]{2,1,0:T(8,128)}) custom-call(f32[3,800,128]{2,1,0:T(8,128)} %get-tuple-element.328.cur_ref, f32[3,8,896]{2,1,0:T(8,128)} %get-tuple-element.329.edges_ref, f32[512,128]{1,0:T(8,128)} %get-tuple-element.330.out_ref), custom_call_target="tpu_custom_call" | custom-call | tf_op jit(solution)/shard_map/pallas_call | solution.py:351
  120.3 0.0 copy-done.3
  120.3 5.3 %conditional.9 = (f32[1,3,1,1,102400]{4,3,2,1,0:T(1,128)}) conditional(s32[]{:T(128)} %convert_element_type.31, (f32[3,800,128]{2,1,0:T(8,128)S(1)}, f32[3,800,128]{2,1,0:T(8,128)S(1)}, f32[2,800,128]{2,1,0:T(8,128)S(1)}, s32[800,128]{1,0:T(8,128)}, f32[3,104,128]{2,1,0:T(8,128)}, /*index=5*/f32[3,104,128]{2,1,0:T(8,128)}, ...), branch_computations={%region_14.15_spmd, %region_15.16_spmd} | conditional | bytes 8 | solution.py:441
  120.4 5.3 %branch_0_fun.9 = (f32[3,800,128]{2,1,0:T(8,128)}, f32[512,128]{1,0:T(8,128)}, f32[3,8,896]{2,1,0:T(8,128)}) custom-call(f32[3,800,128]{2,1,0:T(8,128)S(1)} %get-tuple-element.251.cur_ref, f32[3,800,128]{2,1,0:T(8,128)S(1)} %get-tuple-element.252.prev_ref, f32[2,800,128]{2,1,0:T(8,128)S(1)} %get-tuple-element.253.coef_ref, ...), custom_call_target="tpu_custom_call" | custom-call | tf_op jit(solution)/shard_map/cond/branch_0_fun/pallas_call | solution.py:208
  (7 shorter events, 0.1 us)
Async XLA Ops:
  0.0 8.0 %copy-start = (f32[1,3,1,1,102400]{4,3,2,1,0:T(1,128)S(1)}, f32[1,3,1,1,102400]{4,3,2,1,0:T(1,128)}, u32[]{:S(2)}) copy-start(f32[1,3,1,1,102400]{4,3,2,1,0:T(1,128)} %param.17) | copy-start | bytes 3686404
  11.5 31.7 %copy-start.1 = (f32[1,2,1,1,102400]{4,3,2,1,0:T(1,128)S(1)}, f32[1,2,1,1,102400]{4,3,2,1,0:T(1,128)}, u32[]{:S(2)}) copy-start(f32[1,2,1,1,102400]{4,3,2,1,0:T(1,128)} %param.19) | copy-start | bytes 2457604
  74.4 20.2 %copy-start.2 = (f32[3,800,128]{2,1,0:T(8,128)S(1)}, f32[3,800,128]{2,1,0:T(8,128)}, u32[]{:S(2)}) copy-start(f32[3,800,128]{2,1,0:T(8,128)} %get-tuple-element.320.cur_ref) | copy-start | bytes 3686404
  100.2 20.2 %copy-start.3 = (f32[3,800,128]{2,1,0:T(8,128)S(1)}, f32[3,800,128]{2,1,0:T(8,128)}, u32[]{:S(2)}) copy-start(f32[3,800,128]{2,1,0:T(8,128)} %get-tuple-element.328.cur_ref) | copy-start | bytes 3686404
